TPU v7x, 32 devices: a whole 2x2x4 slice. The times are simulated.
32 devices in a mesh: dp: 8 (over z, x), fsdp: 4 (over y, core).
Axes of the slice: x: 2, y: 2, z: 4, core: 2. Of those that a mesh axis runs over, the one named last changes fastest.
Arguments:
- block_in: float32 [32, 334, 1152], P(('dp', 'fsdp')), may hold values from -6 to 6
- skip_in: float32 [32, 334, 1152], P(('dp', 'fsdp')), may hold values from -6 to 6
- out_grad: float32 [32, 334, 1152], P(('dp', 'fsdp')), may hold values from -6 to 6
- caption_len: int32 [32], P(('dp', 'fsdp')), may hold values from 1 to 77
- skip_w: float32 [2654208], P(('dp', 'fsdp')), may hold values from -0.125 to 0.125
- qkv_w: float32 [3981312], P(('dp', 'fsdp')), may hold values from -0.1875 to 0.1875
- proj_w: float32 [1327104], P(('dp', 'fsdp')), may hold values from -1.5 to 1.5
- fc1_w: float32 [5308416], P(('dp', 'fsdp')), may hold values from -0.1875 to 0.1875
- fc2_w: float32 [5308416], P(('dp', 'fsdp')), may hold values from -0.09375 to 0.09375
- vectors: float32 [12672], P('dp'), may hold values from -0.9 to 1.5
Outputs:
- block_out: float32 [32, 334, 1152], P(('dp', 'fsdp'))
- in_grad: float32 [32, 334, 1152], P(('dp', 'fsdp'))
- skip_grad: float32 [32, 334, 1152], P(('dp', 'fsdp'))
- skip_w_grad: float32 [2654208], P(('dp', 'fsdp'))
- qkv_w_grad: float32 [3981312], P(('dp', 'fsdp'))
- proj_w_grad: float32 [1327104], P(('dp', 'fsdp'))
- fc1_w_grad: float32 [5308416], P(('dp', 'fsdp'))
- fc2_w_grad: float32 [5308416], P(('dp', 'fsdp'))
- vectors_grad: float32 [12672], P('dp')
All inputs are finite; a program needn't handle non-finite values.
Results may differ from a plain program's by a relative error of at most 0.012.
Values may be sent and summed in bfloat16 or wider, within the bound.
A program may use at most 320 MiB of HBM per device.

v0:
```python
import jax
import jax.numpy as jnp
from jax import lax
from jax.sharding import PartitionSpec as P

HEADS = 16
FF = 4608
CAPTION = 77


epsilon = 1e-05
masked_value = -1e30


def norm_rows(value, gain, shift):
    center = value - jnp.mean(value, -1, keepdims=True)
    spread = jnp.mean(center * center, -1, keepdims=True)
    return center * lax.rsqrt(spread + epsilon) * gain + shift


def gelu_exact(value):
    return jax.nn.gelu(value, approximate=False)


def key_valid(caption_len, length, caption):
    place = lax.broadcasted_iota(jnp.int32, (caption_len.shape[0], length), 1)
    return (place < 1 + caption_len[:, None]) | (place >= 1 + caption)


def product(left, right):
    return jnp.dot(left, right, preferred_element_type=jnp.float32)


def left_product(left, right):
    return lax.dot_general(
        left, right, (((0,), (0,)), ((), ())), preferred_element_type=jnp.float32
    )


def right_product(left, right):
    return lax.dot_general(
        left, right, (((1,), (1,)), ((), ())), preferred_element_type=jnp.float32
    )


def unpack(flat, width, hidden):
    return (
        flat[0].reshape(2 * width, width),
        flat[1].reshape(width, 3 * width),
        flat[2].reshape(width, width),
        flat[3].reshape(width, hidden),
        flat[4].reshape(hidden, width),
    )


def attention_scores(query, keys, valid, scale):
    raw = jnp.einsum("ishd,ithd->ihst", query, keys, preferred_element_type=jnp.float32) * scale
    return jnp.where(valid[:, None, None, :], raw, masked_value)


def column_sum(value):
    return jnp.sum(value.astype(jnp.float32), 0)


def flat_piece(left, right):
    grad_rows = left_product(left, right).reshape(-1)
    return grad_rows


def body(block_in, skip_in, out_grad, caption_len, skip_w, qkv_w, proj_w, fc1_w, fc2_w, vectors):
    items, length, width = block_in.shape
    heads = HEADS
    head_dim = width // heads
    hidden = FF
    rows = items * length
    scale = head_dim ** (-0.5)
    gathered = (
        lax.all_gather(skip_w.astype(jnp.bfloat16), ("dp", "fsdp"), axis=0, tiled=True),
        lax.all_gather(qkv_w.astype(jnp.bfloat16), ("dp", "fsdp"), axis=0, tiled=True),
        lax.all_gather(proj_w.astype(jnp.bfloat16), ("dp", "fsdp"), axis=0, tiled=True),
        lax.all_gather(fc1_w.astype(jnp.bfloat16), ("dp", "fsdp"), axis=0, tiled=True),
        lax.all_gather(fc2_w.astype(jnp.bfloat16), ("dp", "fsdp"), axis=0, tiled=True),
    )
    skip_m, qkv_m, proj_m, fc1_m, fc2_m = unpack(gathered, width, hidden)
    vec = lax.all_gather(vectors, "dp", axis=0, tiled=True)
    gain_one = vec[0:width]
    shift_one = vec[width : 2 * width]
    gain_two = vec[2 * width : 3 * width]
    shift_two = vec[3 * width : 4 * width]
    skip_bias = vec[4 * width : 5 * width]
    proj_bias = vec[5 * width : 6 * width]
    fc2_bias = vec[6 * width : 7 * width]
    fc1_bias = vec[7 * width :]
    valid = key_valid(caption_len, length, CAPTION)
    joined = jnp.concatenate([block_in, skip_in], -1).reshape(rows, 2 * width).astype(jnp.bfloat16)
    first = product(joined, skip_m) + skip_bias
    normed_one = norm_rows(first, gain_one, shift_one).astype(jnp.bfloat16)
    triple = (
        product(normed_one, qkv_m).astype(jnp.bfloat16).reshape(items, length, 3, heads, head_dim)
    )
    query = triple[:, :, 0]
    keys = triple[:, :, 1]
    values = triple[:, :, 2]
    scores = attention_scores(query, keys, valid, scale)
    top = jnp.max(scores, -1, keepdims=True)
    expd = jnp.exp(scores - top)
    total = jnp.sum(expd, -1, keepdims=True)
    probs = expd / total
    log_total = top + jnp.log(total)
    mixed = (
        jnp.einsum(
            "ihst,ithd->ishd",
            probs.astype(jnp.bfloat16),
            values,
            preferred_element_type=jnp.float32,
        )
        .astype(jnp.bfloat16)
        .reshape(rows, width)
    )
    second = first + (product(mixed, proj_m) + proj_bias)
    normed_two = norm_rows(second, gain_two, shift_two).astype(jnp.bfloat16)
    inner = product(normed_two, fc1_m) + fc1_bias
    active = gelu_exact(inner).astype(jnp.bfloat16)
    block_out = second + (product(active, fc2_m) + fc2_bias)
    again = (
        lax.all_gather(skip_w.astype(jnp.bfloat16), ("dp", "fsdp"), axis=0, tiled=True),
        lax.all_gather(qkv_w.astype(jnp.bfloat16), ("dp", "fsdp"), axis=0, tiled=True),
        lax.all_gather(proj_w.astype(jnp.bfloat16), ("dp", "fsdp"), axis=0, tiled=True),
        lax.all_gather(fc1_w.astype(jnp.bfloat16), ("dp", "fsdp"), axis=0, tiled=True),
        lax.all_gather(fc2_w.astype(jnp.bfloat16), ("dp", "fsdp"), axis=0, tiled=True),
    )
    skip_m, qkv_m, proj_m, fc1_m, fc2_m = unpack(again, width, hidden)
    grad_out = out_grad.reshape(rows, width)
    grad_mlp = grad_out.astype(jnp.bfloat16)
    d_fc2_bias = column_sum(grad_mlp)
    d_active = right_product(grad_mlp, fc2_m)
    gelu_value, gelu_pull = jax.vjp(gelu_exact, inner)
    grad_inner = gelu_pull(d_active)[0].astype(jnp.bfloat16)
    d_fc1_bias = column_sum(grad_inner)
    d_normed_two = right_product(grad_inner, fc1_m)
    norm_value_two, norm_pull_two = jax.vjp(norm_rows, second, gain_two, shift_two)
    d_second_norm, d_gain_two, d_shift_two = norm_pull_two(d_normed_two)
    grad_second = grad_out + d_second_norm
    grad_attn = grad_second.astype(jnp.bfloat16)
    d_proj_bias = column_sum(grad_attn)
    grad_mixed = (
        right_product(grad_attn, proj_m)
        .astype(jnp.bfloat16)
        .reshape(items, length, heads, head_dim)
    )
    again_scores = attention_scores(query, keys, valid, scale)
    again_probs = jnp.exp(again_scores - log_total)
    d_probs = jnp.einsum("ishd,ithd->ihst", grad_mixed, values, preferred_element_type=jnp.float32)
    inner_sum = jnp.sum(again_probs * d_probs, -1, keepdims=True)
    grad_scores = (again_probs * (d_probs - inner_sum)).astype(jnp.bfloat16)
    d_query = (
        jnp.einsum("ihst,ithd->ishd", grad_scores, keys, preferred_element_type=jnp.float32) * scale
    )
    d_keys = (
        jnp.einsum("ihst,ishd->ithd", grad_scores, query, preferred_element_type=jnp.float32)
        * scale
    )
    d_values = jnp.einsum(
        "ihst,ishd->ithd",
        again_probs.astype(jnp.bfloat16),
        grad_mixed,
        preferred_element_type=jnp.float32,
    )
    grad_triple = (
        jnp.stack([d_query, d_keys, d_values], 2).astype(jnp.bfloat16).reshape(rows, 3 * width)
    )
    d_normed_one = right_product(grad_triple, qkv_m)
    norm_value_one, norm_pull_one = jax.vjp(norm_rows, first, gain_one, shift_one)
    d_first_norm, d_gain_one, d_shift_one = norm_pull_one(d_normed_one)
    grad_first = (grad_second + d_first_norm).astype(jnp.bfloat16)
    d_skip_bias = column_sum(grad_first)
    grad_joined = right_product(grad_first, skip_m).reshape(items, length, 2 * width)
    in_grad = grad_joined[:, :, 0:width]
    skip_grad = grad_joined[:, :, width:]
    owners = lax.axis_size(("dp", "fsdp"))
    pairs = (
        (joined, grad_first),
        (normed_one, grad_triple),
        (mixed, grad_attn),
        (normed_two, grad_inner),
        (active, grad_mlp),
    )
    shard_sizes = [pair[0].shape[1] * pair[1].shape[1] // owners for pair in pairs]
    blocks = []
    for pair, owner_share in zip(pairs, shard_sizes):
        blocks.append(
            flat_piece(pair[0], pair[1]).reshape(1 * lax.axis_size(("dp", "fsdp")), owner_share)
        )
    owned = lax.psum_scatter(
        jnp.concatenate(blocks, 1), ("dp", "fsdp"), scatter_dimension=0, tiled=True
    ).reshape(-1)
    pieces = []
    offset = 0
    for share in shard_sizes:
        pieces.append(owned[offset : offset + share])
        offset = offset + share
    vec_grad = jnp.concatenate(
        [
            d_gain_one,
            d_shift_one,
            d_gain_two,
            d_shift_two,
            d_skip_bias,
            d_proj_bias,
            d_fc2_bias,
            d_fc1_bias,
        ]
    )
    vec_rows = lax.psum_scatter(vec_grad, "dp", scatter_dimension=0, tiled=True)
    vec_total = lax.psum(vec_rows, "fsdp")
    return (
        block_out.reshape(items, length, width),
        in_grad,
        skip_grad,
        pieces[0],
        pieces[1],
        pieces[2],
        pieces[3],
        pieces[4],
        vec_total,
    )


def solution(mesh):
    placed = (
        P(("dp", "fsdp"), None, None),
        P(("dp", "fsdp"), None, None),
        P(("dp", "fsdp"), None, None),
        P(("dp", "fsdp")),
        P(("dp", "fsdp")),
        P(("dp", "fsdp")),
        P(("dp", "fsdp")),
        P(("dp", "fsdp")),
        P(("dp", "fsdp")),
        P("dp"),
    )
    return jax.shard_map(
        body,
        mesh=mesh,
        in_specs=placed,
        out_specs=(
            P(("dp", "fsdp"), None, None),
            P(("dp", "fsdp"), None, None),
            P(("dp", "fsdp"), None, None),
            P(("dp", "fsdp")),
            P(("dp", "fsdp")),
            P(("dp", "fsdp")),
            P(("dp", "fsdp")),
            P(("dp", "fsdp")),
            P("dp"),
        ),
        check_vma=False,
    )
```

profile of v0, /device:TPU:0, one launch (start us, length us, event | category | flops | bytes accessed | tf_op | source)
XLA Modules:
  0.0 1833.7 jit_solution(9964866193865777532)
XLA Ops:
  18.2 3.6 convert.10
  24.1 40.1 %all-reduce = f32[12672]{0:T(1024)S(1)} all-reduce(f32[12672]{0:T(1024)S(1)} %dynamic-update-slice), channel_id=1, replica_groups=mesh['dp'=8,'fsdp'=4] {'dp'}, use_global_device_ids=true, to_apply=%add | all-reduce | flops 12672 | bytes 101376
  68.4 4.9 pad_maximum_fusion
  73.3 6.9 all-gather.16.cloned.1.call-done
  80.1 48.6 %reduce.7 = bf16[32,41472]{1,0:T(8,128)(2,1)} reduce(bf16[32,1,41472]{2,1,0:T(2,128)(2,1)} %all-gather.16.cloned.1.call-done, bf16[]{:T(256)} %constant.106), dimensions={1}, to_apply=%all-gather.1.reduce_sub_computation | reduce | bytes 5308418 | tf_op jit(solution)/shard_map/all_gather | solution.py:80
  128.7 6.4 reshape.318
  135.1 13.0 all-gather.8.cloned.1.call-done
  148.1 11.3 reshape.311
  159.3 5.4 fusion.47
  165.1 96.3 %all-gather.14.cloned.1.call-done = bf16[32,1,124416]{2,1,0:T(2,128)(2,1)} async-done(((bf16[1,1,124416]{2,1,0:T(2,128)(2,1)}), bf16[32,1,124416]{2,1,0:T(2,128)(2,1)}) %all-gather.14.cloned.1.call-update) | async-done | bytes 7962640 | tf_op jit(solution)/shard_map/all_gather | solution.py:79
  261.4 167.2 %reduce.6 = bf16[32,124416]{1,0:T(8,128)(2,1)} reduce(bf16[32,1,124416]{2,1,0:T(2,128)(2,1)} %all-gather.14.cloned.1.call-done, bf16[]{:T(256)} %constant.106), dimensions={1}, to_apply=%all-gather.reduce_sub_computation | reduce | bytes 15925250 | tf_op jit(solution)/shard_map/all_gather | solution.py:79
  428.6 14.9 reshape.312
  443.5 8.0 convolution_convert_fusion
  451.5 4.4 copy.40
  455.9 3.6 fusion.48
  462.7 3.0 fusion.24
  468.7 19.3 %reshape.319 = bf16[1152,4608]{1,0:T(8,128)(2,1)} reshape(bf16[5308416]{0:T(1024)(128)(2,1)} %all-gather.10.cloned.1.call-done) | data formatting | bytes 21233664 | tf_op jit(solution)/shard_map/reshape | solution.py:51
  488.0 22.2 %multiply_convert_fusion.1 = (bf16[334,4608]{1,0:T(8,128)(2,1)}, f32[334,4608]{1,0:T(8,128)}, f32[334,4608]{1,0:T(8,128)}) fusion(f32[4608]{0:T(1024)S(1)} %slice.101, bf16[1152,4608]{1,0:T(8,128)(2,1)} %reshape.319, f32[334,1152]{1,0:T(8,128)} %copy-done.5, f32[1152]{0:T(1024)S(1)} %get-tuple-element.58, f32[1152]{0:T(1024)S(1)} %get-tuple-element.59, ...), kind=kOutput, calls=%fused_computation.13 | convolution fusion | flops 3649524480 | bytes 27576944 | tf_op jit(solution)/shard_map/dot_general | solution.py:31
  510.2 20.4 %reshape.320 = bf16[4608,1152]{1,0:T(8,128)(2,1)} reshape(bf16[5308416]{0:T(1024)(128)(2,1)} %all-gather.12.cloned.1.call-done) | data formatting | bytes 21233664 | tf_op jit(solution)/shard_map/reshape | solution.py:52
  530.6 11.9 convert_reduce_fusion
  542.5 10.1 multiply_reduce_fusion.1
  560.5 5.1 fusion.21
  565.6 4.6 multiply_reduce_fusion
  575.9 4.6 multiply_reduce_fusion.2
  580.5 8.2 fusion.37
  588.8 3.9 fusion.50
  592.7 10.4 fusion.38
  605.5 5.8 fusion.18
  611.3 8.6 reshape_reshape.15
  619.9 8.6 constant_dynamic-update-slice_fusion.4
  628.5 12.5 reshape_reshape.16
  641.0 5.8 reshape_reshape.17
  646.8 30.1 %reshape_reshape.18 = f32[32,165888]{1,0:T(8,128)} reshape(f32[1152,4608]{1,0:T(8,128)} %fusion.38) | data formatting | bytes 42467328 | tf_op jit(solution)/shard_map/reshape;reshape | solution.py:192
  676.9 12.9 fusion.31
  689.8 22.5 %reshape_reshape.19 = f32[32,165888]{1,0:T(8,128)} reshape(f32[4608,1152]{1,0:T(8,128)} %fusion.31) | data formatting | bytes 42467328 | tf_op jit(solution)/shard_map/reshape;reshape | solution.py:192
  712.4 12.9 constant_dynamic-update-slice_fusion.3
  725.3 6.4 constant_dynamic-update-slice_fusion.2
  733.3 7.6 constant_dynamic-update-slice_fusion.1
  740.9 14.9 constant_dynamic-update-slice_fusion
  757.2 10.5 fusion.14
  767.7 2.7 copy.46
  770.4 4.8 convolution_bitcast_fusion
  775.5 2.7 copy.47
  781.0 37.2 %all-reduce.2 = f32[12672]{0:T(1024)S(1)} all-reduce(f32[12672]{0:T(1024)S(1)} %constant_dynamic-update-slice_fusion.6), channel_id=3, replica_groups=mesh['dp'=8,'fsdp'=4] {'dp'}, use_global_device_ids=true, to_apply=%region_20.21.clone | all-reduce | flops 12672 | bytes 101376
  818.3 6.9 psum.7
  825.2 985.5 %all-reduce.5.cloned.1.call-done = f32[32,580608]{1,0:T(8,128)} async-done(((f32[32,580608]{1,0:T(8,128)}), f32[32,580608]{1,0:T(8,128)}) %all-reduce.5.cloned.1.call-update) | async-done | bytes 74317840
  1813.4 4.4 dynamic-slice_reduce_fusion
  1820.3 6.4 fusion.43
  (154 shorter events, 48.8 us)
Async XLA Ops:
  7.2 7.7 copy-start.20
  7.2 73.0 %all-gather.16.cloned.1.call-start = ((), (), s32[]{:S(2)}) async-start(), calls=%async_computation.4 | async-start | bytes 5474304 | tf_op jit(solution)/shard_map/all_gather | solution.py:80
  9.0 139.1 %all-gather.8.cloned.1.call-start = ((), (), s32[]{:S(2)}) async-start(), calls=%async_computation | async-start | bytes 5474304 | tf_op jit(solution)/shard_map/all_gather | solution.py:78
  10.7 250.6 %all-gather.14.cloned.1.call-start = ((), (), s32[]{:S(2)}) async-start(), calls=%async_computation.3 | async-start | bytes 16422912 | tf_op jit(solution)/shard_map/all_gather | solution.py:79
  12.9 455.7 %all-gather.10.cloned.1.call-start = ((), (), s32[]{:S(2)}) async-start(), calls=%async_computation.1 | async-start | bytes 10948608 | tf_op jit(solution)/shard_map/all_gather | solution.py:81
  14.8 7.7 copy-start.31
  14.8 8.9 copy-start.26
  14.8 49.4 %copy-start.1 = (f32[1,334,1152]{2,0,1:T(1,128)S(1)}, f32[1,334,1152]{2,0,1:T(1,128)}, u32[]{:S(2)}) copy-start(f32[1,334,1152]{2,0,1:T(1,128)} %param.12) | copy-start | bytes 4617220
  14.8 495.4 %all-gather.12.cloned.1.call-start = ((), (), s32[]{:S(2)}) async-start(), calls=%async_computation.2 | async-start | bytes 10948608 | tf_op jit(solution)/shard_map/all_gather | solution.py:82
  15.7 1795.0 %all-reduce.5.cloned.1.call-start = ((), (), s32[]{:S(2)}) async-start(), calls=%async_computation.5 | async-start | bytes 148635648
  64.2 2.8 copy-start.9
  165.1 263.5 %copy-start.23 = (f32[334]{0:T(512)}, f32[334]{0:T(512)S(1)}, u32[]{:S(2)}) copy-start(f32[334]{0:T(512)S(1)} %multiply_reduce_fusion.6) | copy-start | bytes 4012
  459.5 3.2 copy-start
  462.7 3.0 copy-start.16
  465.7 2.9 copy-start.18
  467.2 1.1 copy-start.5
  530.6 11.9 copy-start.6
  542.5 10.1 copy-start.12
  552.6 3.4 copy-start.17
  553.2 1.1 copy-start.3
  555.2 0.9 copy-start.14
  560.5 5.2 copy-start.2
  560.5 5.2 copy-start.11
  560.5 9.8 slice-start
  565.6 4.7 slice-start.1
  572.3 2.9 slice-start.8
  573.6 2.3 slice-start.9
  580.5 8.2 copy-start.15
  580.5 8.2 copy-start.19
  588.8 3.9 copy-start.7
  588.8 3.9 copy-start.13
  592.7 10.5 copy-start.24
  603.2 1.4 copy-start.4
  603.2 2.3 copy-start.10
  712.3 19.4 %slice-start.2 = ((s8[21233664]{0:T(1024)(128)(4,1)}), s8[4194304]{0:T(1024)(128)(4,1)S(1)}, s32[]{:S(2)}) async-start(s8[21233664]{0:T(1024)(128)(4,1)} %bitcast.108), calls=%async_computation.8 | async-start | bytes 8388608
  712.3 19.4 %slice-start.3 = ((s8[21233664]{0:T(1024)(128)(4,1)}), s8[4194304]{0:T(1024)(128)(4,1)S(1)}, s32[]{:S(2)}) async-start(s8[21233664]{0:T(1024)(128)(4,1)} %bitcast.108), calls=%async_computation.9 | async-start | bytes 8388608
  712.3 19.4 %slice-start.4 = ((s8[21233664]{0:T(1024)(128)(4,1)}), s8[4194304]{0:T(1024)(128)(4,1)S(1)}, s32[]{:S(2)}) async-start(s8[21233664]{0:T(1024)(128)(4,1)} %bitcast.108), calls=%async_computation.10 | async-start | bytes 8388608
  712.3 19.4 %slice-start.5 = ((s8[21233664]{0:T(1024)(128)(4,1)}), s8[4194304]{0:T(1024)(128)(4,1)S(1)}, s32[]{:S(2)}) async-start(s8[21233664]{0:T(1024)(128)(4,1)} %bitcast.108), calls=%async_computation.11 | async-start | bytes 8388608
  712.3 20.9 %slice-start.6 = ((s8[21233664]{0:T(1024)(128)(4,1)}), s8[4194304]{0:T(1024)(128)(4,1)S(1)}, s32[]{:S(2)}) async-start(s8[21233664]{0:T(1024)(128)(4,1)} %bitcast.108), calls=%async_computation.12 | async-start | bytes 8388608
  725.3 8.0 slice-start.7
  755.8 1.4 copy-start.8
  755.8 1.4 copy-start.25
  775.4 5.5 copy-start.30
  775.4 5.5 copy-start.29
  775.4 5.5 copy-start.28
  775.4 5.5 copy-start.27
  775.4 5.5 copy-start.21
  775.5 5.6 copy-start.22
Sparse Core Ops, SparseCore 0:
  11.4 68.6 all-gather.15
  83.5 64.4 all-gather.7
  151.5 109.8 all-gather.13
  264.7 85.5 all-gather.9
  353.6 85.8 all-gather.11
  756.0 1054.7 all-reduce.4
where the time goes:
time: 1840 us; the launch traced here: 1830 us
  waiting for transfers between devices  1100 us (60%)
  local copies, waits for them, and re-layouts  248 us (13%)
  other arithmetic  242 us (13%)
  matrix products  141 us (8%)
  blocking collectives  84.1 us (5%)
    unnamed x7, waiting for transfers between devices  986 us
    all_gather x1, other arithmetic, body(): lax.all_gather(qkv_w.astype(jnp.bfloat16), ('dp', 'fsdp'), axis=0, tiled=...  167 us
    all_gather x1, waiting for transfers between devices, body(): lax.all_gather(qkv_w.astype(jnp.bfloat16), ('dp', 'fsdp'), axis=0, tiled=...  96.3 us
    another operation x5, local copies, waits for them, and re-layouts, body(): flat_piece(pair[0], pair[1])  79.5 us
    unnamed x2, blocking collectives  77.2 us
    unnamed x105, local copies, waits for them, and re-layouts  57.5 us
    all_gather x1, other arithmetic, body(): lax.all_gather(proj_w.astype(jnp.bfloat16), ('dp', 'fsdp'), axis=0, tiled...  48.6 us
    dot_general x5, matrix products, product(): return jnp.dot(left, right, preferred_element_type=jnp.float32)  47.5 us
  transfers between devices with their start and end apart: 6, of which 4 were waited for; matrix products, arithmetic and copies ran while one was open for 20% of the time, Pallas kernels for 0%

commit v1 on v0

--- a/solution.py
+++ b/solution.py
@@ -1,6 +1,10 @@
+import functools
+
 import jax
 import jax.numpy as jnp
 from jax import lax
+from jax.experimental import pallas as pl
+from jax.experimental.pallas import tpu as pltpu
 from jax.sharding import PartitionSpec as P
 
 HEADS = 16
@@ -41,6 +45,10 @@
     return lax.dot_general(
         left, right, (((1,), (1,)), ((), ())), preferred_element_type=jnp.float32
     )
+
+
+def whole_rows(width, dp, fsdp):
+    return fsdp == 4 and dp % 2 == 0 and width % (dp * 16) == 0
 
 
 def unpack(flat, width, hidden):
@@ -67,6 +75,152 @@
     return grad_rows
 
 
+MESH = pl.DeviceIdType.MESH
+BF=jnp.bfloat16; F32=jnp.float32
+
+def gather_kernel(Z, wide, rows, lanes_a,
+                  skip_ref, qkv_ref, proj_ref, fc1_ref, fc2_ref, vec_ref,
+                  skip_o, qp_o, fc1_o, fc2_o, vec_o,
+                  own, mine, give, take, send, recv, lsem, psend, precv, vsend, vrecv):
+    dp = lax.axis_index("dp"); f = lax.axis_index("fsdp")
+    z = dp // 2; x = dp % 2; y = f // 2; c = f % 2
+    nt = wide // 128
+    half = rows // 2
+    A = pl.ds(0, lanes_a); C = pl.ds(lanes_a, wide - lanes_a)
+    zs = [(lax.rem(z + k, Z) * 2 + x, f) for k in range(1, Z)]
+    xp = (z * 2 + 1 - x, f)
+    yp = (dp, (1 - y) * 2 + c)
+    pp = (dp, y * 2 + 1 - c)
+    ndp = 2 * Z
+    others = [(lax.rem(dp + k, ndp), f) for k in range(1, ndp)]
+    bar = pltpu.get_barrier_semaphore()
+    for d in others + [yp, pp]:
+        pl.semaphore_signal(bar, inc=1, device_id=d, device_id_type=MESH)
+    for j in range(nt):
+        cols = slice(128 * j, 128 * j + 128)
+        own[0, :, cols] = skip_ref[pl.ds(j, rows, stride=nt), :].astype(BF)
+        own[5, :, cols] = fc2_ref[pl.ds(j, rows, stride=nt), :].astype(BF)
+        own[6, :, cols] = fc2_ref[pl.ds(j + nt * rows, rows, stride=nt), :].astype(BF)
+        q = [qkv_ref[pl.ds(nt * v + j, half, stride=3 * nt), :] for v in range(3)]
+        q.append(proj_ref[pl.ds(j, half, stride=nt), :])
+        g = [fc1_ref[pl.ds(nt * v + j, half, stride=4 * nt), :] for v in range(4)]
+        four = q + g
+        for i in range(4):
+            a, b = four[2 * i], four[2 * i + 1]
+            mine[i, 0:half, cols] = jnp.where(c == 0, a, b)
+            give[i, 0:half, cols] = jnp.where(c == 0, b, a).astype(BF)
+    pl.semaphore_wait(bar, len(others) + 2)
+    vcopies = []
+    for k, d in enumerate(others):
+        cp = pltpu.make_async_remote_copy(vec_ref, vec_o.at[dp], vsend.at[k], vrecv.at[k], device_id=d, device_id_type=MESH)
+        cp.start(); vcopies.append(cp)
+    lv = pltpu.make_async_copy(vec_ref, vec_o.at[dp], lsem.at[7])
+    lv.start()
+    pc = [pltpu.make_async_remote_copy(give.at[i], take.at[i], psend.at[i], precv.at[i], device_id=pp, device_id_type=MESH) for i in range(4)]
+    for cp in pc: cp.start()
+
+    def unit(i, cc):
+        if i == 0: return skip_o.at[:, :, :, cc]
+        if i in (1, 2): return qp_o.at[2 * (i - 1) + cc]
+        if i in (3, 4): return fc1_o.at[2 * (i - 3) + cc]
+        return fc2_o.at[:, :, :, 2 * cc + (i - 5)]
+    nz = Z - 1
+    waits = []
+    def rc(i, slot, src, dst, dev):
+        cp = pltpu.make_async_remote_copy(src, dst, send.at[i, slot], recv.at[i, slot], device_id=dev, device_id_type=MESH)
+        cp.start(); waits.append(cp)
+    def got(i, slot, dst):
+        pltpu.make_async_remote_copy(dst, dst, send.at[i, slot], recv.at[i, slot], device_id=pp, device_id_type=MESH).wait_recv()
+    def stage1(i):
+        U = unit(i, c)
+        if i in (1, 2, 3, 4):
+            pc[i - 1].wait_recv()
+            a = mine[i - 1, 0:half, :]
+            b = take[i - 1, :, :].astype(F32)[0:half]
+            lo = jnp.where(c == 0, a, b); hi = jnp.where(c == 0, b, a)
+            own[i, :, :] = jnp.concatenate([lo, hi], 0).astype(BF)
+        lc = pltpu.make_async_copy(own.at[i], U.at[z, x, y], lsem.at[i]); lc.start()
+        rc(i, 2 * nz, own.at[i, :, C], U.at[z, x, y, :, C], yp)
+        for k in range(1, Z):
+            rc(i, k - 1, own.at[i, :, A], U.at[z, x, y, :, A], zs[k - 1])
+        return lc
+    def stage2(i, lc):
+        U = unit(i, c)
+        lc.wait()
+        got(i, 2 * nz, U.at[z, x, 1 - y, :, C])
+        for k in range(1, Z):
+            rc(i, nz + k - 1, U.at[z, x, :, :, C], U.at[z, x, :, :, C], zs[k - 1])
+        for k in range(1, Z):
+            got(i, k - 1, U.at[lax.rem(z - k + Z, Z), x, y, :, A])
+        L = U.at[:, x, y, :, A]
+        rc(i, 2 * nz + 1, L, L, xp)
+        rc(i, 2 * nz + 2, L, L, yp)
+        rc(i, 2 * nz + 5, L, L, pp)
+    def stage3(i):
+        U = unit(i, c)
+        for k in range(1, Z):
+            got(i, nz + k - 1, U.at[lax.rem(z - k + Z, Z), x, :, :, C])
+        L = U.at[:, x, :, :, C]
+        rc(i, 2 * nz + 4, L, L, xp)
+        rc(i, 2 * nz + 6, L, L, pp)
+        L = U.at[:, 1 - x, y, :, A]
+        got(i, 2 * nz + 1, L)
+        rc(i, 2 * nz + 3, L, L, yp)
+        rc(i, 2 * nz + 7, L, L, pp)
+    def stage4(i):
+        U = unit(i, c)
+        L = U.at[:, x, 1 - y, :, A]
+        got(i, 2 * nz + 2, L); rc(i, 2 * nz + 8, L, L, pp)
+        L = U.at[:, 1 - x, 1 - y, :, A]
+        got(i, 2 * nz + 3, L); rc(i, 2 * nz + 9, L, L, pp)
+        L = U.at[:, 1 - x, :, :, C]
+        got(i, 2 * nz + 4, L); rc(i, 2 * nz + 10, L, L, pp)
+    def arrived(i):
+        U = unit(i, 1 - c)
+        got(i, 2 * nz + 5, U.at[:, x, y, :, A])
+        got(i, 2 * nz + 7, U.at[:, 1 - x, y, :, A])
+        got(i, 2 * nz + 8, U.at[:, x, 1 - y, :, A])
+        got(i, 2 * nz + 9, U.at[:, 1 - x, 1 - y, :, A])
+        got(i, 2 * nz + 6, U.at[:, x, :, :, C])
+        got(i, 2 * nz + 10, U.at[:, 1 - x, :, :, C])
+    lc = {}
+    lc[0] = stage1(0)
+    for i in range(7):
+        stage2(i, lc[i])
+        if i < 6: lc[i + 1] = stage1(i + 1)
+        stage3(i)
+        if i > 0: stage4(i - 1)
+    stage4(6)
+    for i in range(7): arrived(i)
+    for cp in waits: cp.wait_send()
+    for cp in pc: cp.wait_send()
+    lv.wait()
+    for k, cp in enumerate(vcopies):
+        cp.wait_send()
+        pltpu.make_async_remote_copy(vec_ref, vec_o.at[lax.rem(dp - (k + 1) + ndp, ndp)], vsend.at[k], vrecv.at[k], device_id=pp, device_id_type=MESH).wait_recv()
+
+def gather(skip, qkv, proj, fc1, fc2, vectors, dpn, wide):
+    Z = dpn // 2; rows = skip.shape[0] // wide
+    lanes_a = (wide // 128 * 2 + 1) // 3 * 128
+    U = (Z, 2, 2, rows, wide)
+    hbm = pl.BlockSpec(memory_space=pl.ANY); vm = pl.BlockSpec(memory_space=pltpu.VMEM)
+    ns = 2 * (Z - 1) + 11
+    nv = vectors.shape[0]
+    D = pltpu.SemaphoreType.DMA
+    half = -(-rows // 2 // 16) * 16
+    return pl.pallas_call(
+        functools.partial(gather_kernel, Z, wide, rows, lanes_a),
+        out_shape=(jax.ShapeDtypeStruct((Z, 2, 2, 2, rows, wide), BF), jax.ShapeDtypeStruct((4,) + U, BF),
+                   jax.ShapeDtypeStruct((4,) + U, BF), jax.ShapeDtypeStruct((Z, 2, 2, 4, rows, wide), BF),
+                   jax.ShapeDtypeStruct((dpn, 1, nv), F32)),
+        in_specs=[vm] * 6, out_specs=(hbm,) * 5,
+        scratch_shapes=[pltpu.VMEM((7, rows, wide), BF), pltpu.VMEM((4, half, wide), F32), pltpu.VMEM((4, half, wide), BF), pltpu.VMEM((4, half, wide), BF),
+                        D((7, ns)), D((7, ns)), D((8,)), D((4,)), D((4,)), D((dpn - 1,)), D((dpn - 1,))],
+        compiler_params=pltpu.CompilerParams(collective_id=0, has_side_effects=True, vmem_limit_bytes=32 << 20),
+        name="gather",
+    )(*(w.reshape(-1, 128) for w in (skip, qkv, proj, fc1, fc2)), vectors.reshape(1, nv))
+
+
 def body(block_in, skip_in, out_grad, caption_len, skip_w, qkv_w, proj_w, fc1_w, fc2_w, vectors):
     items, length, width = block_in.shape
     heads = HEADS
@@ -74,15 +228,25 @@
     hidden = FF
     rows = items * length
     scale = head_dim ** (-0.5)
-    gathered = (
-        lax.all_gather(skip_w.astype(jnp.bfloat16), ("dp", "fsdp"), axis=0, tiled=True),
-        lax.all_gather(qkv_w.astype(jnp.bfloat16), ("dp", "fsdp"), axis=0, tiled=True),
-        lax.all_gather(proj_w.astype(jnp.bfloat16), ("dp", "fsdp"), axis=0, tiled=True),
-        lax.all_gather(fc1_w.astype(jnp.bfloat16), ("dp", "fsdp"), axis=0, tiled=True),
-        lax.all_gather(fc2_w.astype(jnp.bfloat16), ("dp", "fsdp"), axis=0, tiled=True),
-    )
-    skip_m, qkv_m, proj_m, fc1_m, fc2_m = unpack(gathered, width, hidden)
-    vec = lax.all_gather(vectors, "dp", axis=0, tiled=True)
+    owners = lax.axis_size(("dp", "fsdp"))
+    if whole_rows(width, lax.axis_size("dp"), lax.axis_size("fsdp")):
+        skip_u, qp_u, fc1_u, fc2_u, vec = gather(
+            skip_w, qkv_w, proj_w, fc1_w, fc2_w, vectors, lax.axis_size("dp"), width
+        )
+        skip_m = skip_u.reshape(2 * width, width)
+        qp_u = qp_u.reshape(4, width, width)
+        qkv_m = jnp.concatenate([qp_u[0], qp_u[1], qp_u[2]], 1)
+        proj_m = qp_u[3]
+        fc1_m = jnp.concatenate([t.reshape(width, width) for t in fc1_u], 1)
+        fc2_m = fc2_u.reshape(hidden, width)
+        vec = vec.reshape(-1)
+    else:
+        gathered = tuple(
+            lax.all_gather(w.astype(jnp.bfloat16), ("dp", "fsdp"), axis=0, tiled=True)
+            for w in (skip_w, qkv_w, proj_w, fc1_w, fc2_w)
+        )
+        skip_m, qkv_m, proj_m, fc1_m, fc2_m = unpack(gathered, width, hidden)
+        vec = lax.all_gather(vectors, "dp", axis=0, tiled=True)
     gain_one = vec[0:width]
     shift_one = vec[width : 2 * width]
     gain_two = vec[2 * width : 3 * width]
@@ -122,14 +286,6 @@
     inner = product(normed_two, fc1_m) + fc1_bias
     active = gelu_exact(inner).astype(jnp.bfloat16)
     block_out = second + (product(active, fc2_m) + fc2_bias)
-    again = (
-        lax.all_gather(skip_w.astype(jnp.bfloat16), ("dp", "fsdp"), axis=0, tiled=True),
-        lax.all_gather(qkv_w.astype(jnp.bfloat16), ("dp", "fsdp"), axis=0, tiled=True),
-        lax.all_gather(proj_w.astype(jnp.bfloat16), ("dp", "fsdp"), axis=0, tiled=True),
-        lax.all_gather(fc1_w.astype(jnp.bfloat16), ("dp", "fsdp"), axis=0, tiled=True),
-        lax.all_gather(fc2_w.astype(jnp.bfloat16), ("dp", "fsdp"), axis=0, tiled=True),
-    )
-    skip_m, qkv_m, proj_m, fc1_m, fc2_m = unpack(again, width, hidden)
     grad_out = out_grad.reshape(rows, width)
     grad_mlp = grad_out.astype(jnp.bfloat16)
     d_fc2_bias = column_sum(grad_mlp)
@@ -177,7 +333,6 @@
     grad_joined = right_product(grad_first, skip_m).reshape(items, length, 2 * width)
     in_grad = grad_joined[:, :, 0:width]
     skip_grad = grad_joined[:, :, width:]
-    owners = lax.axis_size(("dp", "fsdp"))
     pairs = (
         (joined, grad_first),
         (normed_one, grad_triple),

time: 1840 us -> 1570 us (0.85)
  other arithmetic: 242 us -> 13.2 us
  Pallas kernels: 0 us -> 166 us
  waiting for transfers between devices: 1100 us -> 985 us
  local copies, waits for them, and re-layouts: 248 us -> 197 us
  blocking collectives: 84.1 us -> 49.1 us
    all_gather x2 -> x0, other arithmetic: 216 us -> none  [the longest x1 167 us: body(): lax.all_gather(qkv_w.astype(jnp.bfloat16), ('dp', 'fsdp'), axis=0, tiled=...]
    pallas_call x0 -> x1, Pallas kernels: none -> 166 us  [gather(): pl.pallas_call(functools.partial(gather_kernel, Z, wide, rows, lanes_a),...]
    all_gather x5 -> x0, waiting for transfers between devices: 116 us -> none  [the longest x1 96.3 us: body(): lax.all_gather(qkv_w.astype(jnp.bfloat16), ('dp', 'fsdp'), axis=0, tiled=...]
    reshape x5 -> x2, local copies, waits for them, and re-layouts: 72.3 us -> 0.79 us  [the longest x1 0.7 us: gather(): vectors.reshape(1, nv)]
    unnamed x2 -> x1, blocking collectives: 77.2 us -> 42.1 us
    unnamed x105 -> x141, local copies, waits for them, and re-layouts: 57.5 us -> 68.7 us
    unnamed x7 -> x2, waiting for transfers between devices: 986 us -> 985 us
  transfers between devices with their start and end apart: 6 -> 1, of which waited for: 4 -> 1; matrix products, arithmetic and copies ran while one was open for 20% -> 1% of each run, Pallas kernels for 0% -> 0%
where the time goes in v1:
time: 1570 us
  waiting for transfers between devices  985 us (63%)
  local copies, waits for them, and re-layouts  197 us (13%)
  Pallas kernels  166 us (11%)
  matrix products  139 us (9%)
  blocking collectives  49.1 us (3%)
  between operations  16.3 us (1%)
    unnamed x2, waiting for transfers between devices  985 us
    pallas_call x1, Pallas kernels, gather(): pl.pallas_call(functools.partial(gather_kernel, Z, wide, rows, lanes_a),...  166 us
    another operation x5, local copies, waits for them, and re-layouts, body(): flat_piece(pair[0], pair[1])  79.4 us
    unnamed x141, local copies, waits for them, and re-layouts  68.7 us
    dot_general x5, matrix products, product(): return jnp.dot(left, right, preferred_element_type=jnp.float32)  46.2 us
    unnamed x1, blocking collectives  42.1 us
    dot_general x5, matrix products, left_product(): lax.dot_general(left, right, (((0,), (0,)), ((), ())), preferred_element_...  41.4 us
    dot_general x5, matrix products, right_product(): lax.dot_general(left, right, (((1,), (1,)), ((), ())), preferred_element_...  35.3 us
  transfers between devices with their start and end apart: 1, of which 1 were waited for; matrix products, arithmetic and copies ran while one was open for 1% of the time, Pallas kernels for 0%

profile of v1, /device:TPU:0, one launch (start us, length us, event | category | flops | bytes accessed | tf_op | source)
XLA Modules:
  0.0 1565.5 jit_solution(13964181120707194596)
XLA Ops:
  13.0 165.9 %gather.1 = (bf16[4,2,2,2,72,1152]{5,4,3,2,1,0:T(8,128)(2,1)S(1)}, bf16[4,4,2,2,72,1152]{5,4,3,2,1,0:T(8,128)(2,1)S(1)}, bf16[4,4,2,2,72,1152]{5,4,3,2,1,0:T(8,1...) custom-call(f32[648,128]{1,0:T(8,128)S(1)} %bitcast.123, f32[972,128]{1,0:T(8,128)S(1)} %bitcast.122, ...), custom_call_target="tpu_custom_call" | custom-call | tf_op jit(solution)/shard_map/gather/pallas_call | solution.py:211
  179.0 3.9 copy-done
  182.8 2.3 copy-done.6
  189.2 2.3 fusion.56
  193.2 9.8 fusion.52
  203.0 8.6 convolution_convert_fusion
  211.6 4.7 copy.40
  216.9 2.2 fusion.57
  220.4 1.9 copy-done.7
  222.4 1.7 fusion.26
  229.2 24.7 %multiply_convert_fusion.1 = (bf16[334,4608]{1,0:T(8,128)(2,1)}, f32[334,4608]{1,0:T(8,128)}, f32[334,4608]{1,0:T(8,128)}) fusion(f32[4608]{0:T(1024)S(1)} %slice.121, bf16[1152,1152]{1,0:T(8,128)(2,1)S(1)} %bitcast.152, bf16[1152,1152]{1,0:T(8,128)(2,1)S(1)} %bitcast.154, bf16[1152,1152]{1,0:T(8,128)(2,1)S(1)} %bitcast.156, ...), kind=kOutput, calls=%fused_computation.16 | convolution fusion | flops 3691991808 | bytes 27576944 | tf_op jit(solution)/shard_map/dot_general | solution.py:35
  253.9 15.7 %convert_reduce_fusion = (f32[4608]{0:T(1024)}, bf16[334,4608]{1,0:T(8,128)(2,1)S(1)}) fusion(f32[334,4608]{1,0:T(8,128)} %get-tuple-element.61, f32[334,4608]{1,0:T(8,128)} %get-tuple-element.88, bf16[4608,1152]{1,0:T(8,128)(2,1)} %bitcast.163, bf16[1,334,1152]{2,0,1:T(2,128)(2,1)S(1)} %convert_element_type.88), kind=kOutput, calls=%fused_computation.14 | convolution fusion | flops 3570642432 | bytes 26795520 | tf_op jit(solution)/shard_map/dot_general | solution.py:45
  269.6 4.9 multiply_reduce_fusion.1
  276.9 2.2 convolution_convert_fusion.1
  279.1 2.2 copy.42
  281.3 5.1 fusion.27
  286.5 4.6 multiply_reduce_fusion
  291.2 1.9 multiply_convert_fusion
  296.3 3.2 pad_maximum_fusion.4
  300.9 7.6 multiply_reduce_fusion.2
  308.5 8.3 fusion.45
  316.8 3.9 fusion.59
  320.7 10.7 fusion.46
  333.3 5.8 fusion.20
  339.1 8.6 reshape_reshape.15
  347.7 8.6 constant_dynamic-update-slice_fusion.4
  356.3 12.4 reshape_reshape.16
  368.7 5.8 reshape_reshape.17
  374.6 30.0 %reshape_reshape.18 = f32[32,165888]{1,0:T(8,128)} reshape(f32[1152,4608]{1,0:T(8,128)} %fusion.46) | data formatting | bytes 42467328 | tf_op jit(solution)/shard_map/reshape;reshape | solution.py:347
  404.6 12.7 fusion.35
  417.3 22.5 %reshape_reshape.19 = f32[32,165888]{1,0:T(8,128)} reshape(f32[4608,1152]{1,0:T(8,128)} %fusion.35) | data formatting | bytes 42467328 | tf_op jit(solution)/shard_map/reshape;reshape | solution.py:347
  439.8 12.9 constant_dynamic-update-slice_fusion.3
  452.7 6.4 constant_dynamic-update-slice_fusion.2
  459.2 1.5 slice-done.11
  460.7 7.5 constant_dynamic-update-slice_fusion.1
  468.2 14.9 constant_dynamic-update-slice_fusion
  484.6 9.2 fusion.15
  493.7 2.7 copy.46
  496.5 4.9 convolution_bitcast_fusion.1
  501.6 2.7 copy.47
  504.3 2.7 copy.48
  508.5 42.1 %all-reduce.1 = f32[12672]{0:T(1024)S(1)} all-reduce(f32[12672]{0:T(1024)S(1)} %constant_dynamic-update-slice_fusion.6), channel_id=3, replica_groups=mesh['dp'=8,'fsdp'=4] {'dp'}, use_global_device_ids=true, to_apply=%region_20.21.clone | all-reduce | flops 12672 | bytes 101376
  550.7 7.0 psum.7
  557.7 984.7 %all-reduce.4.cloned.1.call-done = f32[32,580608]{1,0:T(8,128)} async-done(((f32[32,580608]{1,0:T(8,128)}), f32[32,580608]{1,0:T(8,128)}) %all-reduce.4.cloned.1.call-update) | async-done | bytes 74317840
  1542.4 2.7 constant_dynamic-slice_fusion
  1545.1 4.4 dynamic-slice_reduce_fusion
  1549.5 2.5 dynamic-slice_reduce_fusion.1
  1552.0 6.4 fusion.51
  (168 shorter events, 29.2 us)
Async XLA Ops:
  7.2 1535.3 %all-reduce.4.cloned.1.call-start = ((), (), s32[]{:S(2)}) async-start(), calls=%async_computation | async-start | bytes 148635648
  13.0 172.9 %copy-start.35 = (f32[1,334,1152]{2,0,1:T(1,128)S(1)}, f32[1,334,1152]{2,0,1:T(1,128)}, u32[]{:S(2)}) copy-start(f32[1,334,1152]{2,0,1:T(1,128)} %param.11) | copy-start | bytes 4617220
  13.0 174.0 %copy-start.36 = (f32[1,334,1152]{2,0,1:T(1,128)S(1)}, f32[1,334,1152]{2,0,1:T(1,128)}, u32[]{:S(2)}) copy-start(f32[1,334,1152]{2,0,1:T(1,128)} %param.10) | copy-start | bytes 4617220
  179.0 3.9 copy-start
  182.8 2.3 copy-start.6
  185.9 17.0 %copy-start.37 = (f32[1152]{0:T(1024)}, f32[1152]{0:T(1024)S(1)}, u32[]{:S(2)}) copy-start(f32[1152]{0:T(1024)S(1)} %get-tuple-element.79) | copy-start | bytes 13828
  186.0 2.6 slice-start.3
  187.1 2.1 slice-start.4
  188.1 3.4 copy-start.19
  188.4 4.6 slice-start
  189.2 3.8 slice-start.1
  189.2 4.0 slice-start.2
  193.0 10.0 copy-start.41
  216.3 4.1 copy-start.9
  219.2 3.2 copy-start.7
  222.4 2.2 copy-start.28
  222.4 5.1 copy-start.32
  224.1 1.9 copy-start.33
  224.6 2.9 copy-start.30
  224.6 3.8 copy-start.31
  226.0 48.5 %copy-start.14 = (f32[334,1152]{1,0:T(8,128)}, f32[334,1152]{1,0:T(8,128)S(1)}, u32[]{:S(2)}) copy-start(f32[334,1152]{1,0:T(8,128)S(1)} %get-tuple-element.87) | copy-start | bytes 4617220
  226.0 3.2 copy-start.29
  269.6 4.9 copy-start.22
  281.3 5.2 copy-start.10
  281.3 5.2 copy-start.21
  281.3 9.8 slice-start.5
  286.5 4.7 slice-start.6
  294.5 1.9 copy-start.20
  300.9 7.6 copy-start.38
  308.5 8.3 copy-start.25
  308.5 8.3 copy-start.34
  316.8 3.9 copy-start.15
  316.8 3.9 copy-start.23
  320.7 10.7 copy-start.42
  439.8 19.4 %slice-start.7 = ((s8[21233664]{0:T(1024)(128)(4,1)}), s8[4194304]{0:T(1024)(128)(4,1)S(1)}, s32[]{:S(2)}) async-start(s8[21233664]{0:T(1024)(128)(4,1)} %bitcast.131), calls=%async_computation.8 | async-start | bytes 8388608
  439.8 19.4 %slice-start.8 = ((s8[21233664]{0:T(1024)(128)(4,1)}), s8[4194304]{0:T(1024)(128)(4,1)S(1)}, s32[]{:S(2)}) async-start(s8[21233664]{0:T(1024)(128)(4,1)} %bitcast.131), calls=%async_computation.9 | async-start | bytes 8388608
  439.8 19.4 %slice-start.9 = ((s8[21233664]{0:T(1024)(128)(4,1)}), s8[4194304]{0:T(1024)(128)(4,1)S(1)}, s32[]{:S(2)}) async-start(s8[21233664]{0:T(1024)(128)(4,1)} %bitcast.131), calls=%async_computation.10 | async-start | bytes 8388608
  439.8 19.4 %slice-start.10 = ((s8[21233664]{0:T(1024)(128)(4,1)}), s8[4194304]{0:T(1024)(128)(4,1)S(1)}, s32[]{:S(2)}) async-start(s8[21233664]{0:T(1024)(128)(4,1)} %bitcast.131), calls=%async_computation.11 | async-start | bytes 8388608
  439.8 20.9 %slice-start.11 = ((s8[21233664]{0:T(1024)(128)(4,1)}), s8[4194304]{0:T(1024)(128)(4,1)S(1)}, s32[]{:S(2)}) async-start(s8[21233664]{0:T(1024)(128)(4,1)} %bitcast.131), calls=%async_computation.12 | async-start | bytes 8388608
  452.7 8.0 slice-start.12
  484.6 11.9 copy-start.27
  501.5 5.5 copy-start.48
  501.6 6.7 copy-start.47
  501.6 6.8 copy-start.46
  501.6 6.8 copy-start.45
  501.6 6.8 copy-start.44
  501.6 6.8 copy-start.39
  501.6 6.8 copy-start.40
  (15 other events, 18.6 us)
Sparse Core Ops, SparseCore 0:
  483.3 1059.0 all-reduce.3

commit v2 on v1

--- a/solution.py
+++ b/solution.py
@@ -45,10 +45,6 @@
     return lax.dot_general(
         left, right, (((1,), (1,)), ((), ())), preferred_element_type=jnp.float32
     )
-
-
-def whole_rows(width, dp, fsdp):
-    return fsdp == 4 and dp % 2 == 0 and width % (dp * 16) == 0
 
 
 def unpack(flat, width, hidden):
@@ -221,32 +217,372 @@
     )(*(w.reshape(-1, 128) for w in (skip, qkv, proj, fc1, fc2)), vectors.reshape(1, nv))
 
 
+def scatter_kernel(Z, wide, rows, lanes_a, length,
+                   z_ref, gm_ref, m_ref, gu_ref, o_ref, ga_ref, n_ref, t_ref, j_ref, g_ref, vec_ref,
+                   skip_o, qkv_o, proj_o, fc1_o, fc2_o, vec_o,
+                   left, right, part, ra1, ra2, ra3, rc1, rc2, rc3, keep, give, take, vgot, vall,
+                   lsem, xsend, xrecv, send, recv, psend, precv, vsend, vrecv, wsend, wrecv):
+    dp = lax.axis_index("dp"); f = lax.axis_index("fsdp")
+    z = dp // 2; x = dp % 2; y = f // 2; c = f % 2
+    nt = wide // 128
+    half = rows // 2
+    A = pl.ds(0, lanes_a); C = pl.ds(lanes_a, wide - lanes_a)
+    zi = [lax.rem(z + k, Z) for k in range(1, Z)]
+    zs = [(t * 2 + x, f) for t in zi]
+    xp = (z * 2 + 1 - x, f)
+    yp = (dp, (1 - y) * 2 + c)
+    pp = (dp, y * 2 + 1 - c)
+    ndp = 2 * Z
+    dps = [(lax.rem(dp + k, ndp), f) for k in range(1, ndp)]
+    fs = [(dp, lax.rem(f + k, 4)) for k in range(1, 4)]
+    bar = pltpu.get_barrier_semaphore()
+    for d in dps + fs:
+        pl.semaphore_signal(bar, inc=1, device_id=d, device_id_type=MESH)
+    pl.semaphore_wait(bar, len(dps) + len(fs))
+
+    def cols(ref, unit):
+        return ref.at[:, pl.ds(pl.multiple_of(unit * wide, 128), wide)]
+    own_rows = pl.ds(0, length); other_rows = pl.ds(length, length)
+    copies = {}
+    def pair(n, src_own, src_other, dst):
+        a = pltpu.make_async_copy(src_own, dst.at[own_rows], lsem.at[n])
+        b = pltpu.make_async_remote_copy(src_other, dst.at[other_rows], xsend.at[n], xrecv.at[n], device_id=pp, device_id_type=MESH)
+        a.start(); b.start()
+        return a, b
+    o = 1 - c
+    copies[0] = pair(0, cols(z_ref, 2 * c), cols(z_ref, 2 * o), left.at[0])
+    copies[1] = pair(1, gm_ref, gm_ref, right.at[0])
+    copies[2] = pair(2, cols(z_ref, 2 * c + 1), cols(z_ref, 2 * o + 1), left.at[1])
+    copies[3] = pair(3, m_ref, m_ref, left.at[2])
+    copies[4] = pair(4, cols(gu_ref, c), cols(gu_ref, o), right.at[1])
+    copies[5] = pair(5, cols(gu_ref, 2 + c), cols(gu_ref, 2 + o), right.at[2])
+    @pl.when(c == 0)
+    def _():
+        pair(6, n_ref, o_ref, left.at[3])
+        pair(7, cols(t_ref, 2), ga_ref, right.at[3])
+    @pl.when(c == 1)
+    def _():
+        pair(6, o_ref, n_ref, left.at[3])
+        pair(7, ga_ref, cols(t_ref, 2), right.at[3])
+    for n, dst in ((6, left.at[3]), (7, right.at[3])):
+        copies[n] = (
+            pltpu.make_async_copy(g_ref, dst.at[own_rows], lsem.at[n]),
+            pltpu.make_async_remote_copy(g_ref, dst.at[other_rows], xsend.at[n], xrecv.at[n], device_id=pp, device_id_type=MESH),
+        )
+    copies[8] = pair(8, n_ref, n_ref, left.at[4])
+    copies[9] = pair(9, cols(t_ref, c), cols(t_ref, o), right.at[4])
+    copies[10] = pair(10, cols(j_ref, c), cols(j_ref, o), left.at[5])
+    copies[11] = pair(11, g_ref, g_ref, right.at[5])
+    need = [(0, 1), (2,), (3, 4), (5,), (6, 7), (8, 9), (10, 11)]
+    which = [(0, 0), (1, 0), (2, 1), (2, 2), (3, 3), (4, 4), (5, 5)]
+
+    vcopies = []
+    for k, d in enumerate(dps):
+        cp = pltpu.make_async_remote_copy(vec_ref.at[d[0]], vgot.at[k], vsend.at[k], vrecv.at[k], device_id=d, device_id_type=MESH)
+        cp.start(); vcopies.append(cp)
+
+    started = {j: [] for j in range(7)}
+    def rc(j, slot, src, dst, dev):
+        cp = pltpu.make_async_remote_copy(src, dst, send.at[j, slot], recv.at[j, slot], device_id=dev, device_id_type=MESH)
+        cp.start(); started[j].append(cp)
+    def got(j, slot, dst):
+        pltpu.make_async_remote_copy(dst, dst, send.at[j, slot], recv.at[j, slot], device_id=pp, device_id_type=MESH).wait_recv()
+    nz = Z - 1
+    nb = part.shape[0]
+
+    def stage1(j):
+        for n in need[j]:
+            copies[n][0].wait(); copies[n][1].wait_recv()
+        if j >= nb:
+            for cp in started[j - nb]: cp.wait_send()
+        D = part.at[j % nb]
+        li, ri = which[j]
+        step = wide - lanes_a
+        def chunk(n, _):
+            lanes = pl.ds(pl.multiple_of(n * step, 128), step)
+            r = lax.dot_general(left[li], right[ri, :, lanes], (((0,), (0,)), ((), ())), preferred_element_type=F32)
+            D[:, :, :, :, lanes] = r.reshape(Z, 2, 2, rows, step).astype(BF)
+            return _
+        lax.fori_loop(0, wide // step, chunk, 0)
+        rc(j, 0, D.at[:, 1 - x, 1 - y, :, A], ra1.at[j, 0], yp)
+        rc(j, 2, D.at[:, 1 - x, :, :, C], rc1.at[j], xp)
+        rc(j, 1, D.at[:, x, 1 - y, :, A], ra1.at[j, 1], yp)
+    def add(D, at, got_ref):
+        D[at] = (D[at].astype(F32) + got_ref[...].astype(F32)).astype(BF)
+    def stage2(j):
+        D = part.at[j % nb]
+        got(j, 0, ra1.at[j, 0])
+        for zz in range(Z):
+            va = D.at[zz, 1 - x, y, :, A]
+            va[...] = (va[...].astype(F32) + ra1[j, 0, zz].astype(F32)).astype(BF)
+        rc(j, 3, D.at[:, 1 - x, y, :, A], ra2.at[j], xp)
+        got(j, 2, rc1.at[j])
+        for zz in range(Z):
+            for yy in range(2):
+                va = D.at[zz, x, yy, :, C]
+                va[...] = (va[...].astype(F32) + rc1[j, zz, yy].astype(F32)).astype(BF)
+        for k in range(nz):
+            rc(j, 4 + k, D.at[zi[k], x, :, :, C], rc2.at[j, k], zs[k])
+    def stage3(j):
+        D = part.at[j % nb]
+        got(j, 1, ra1.at[j, 1])
+        got(j, 3, ra2.at[j])
+        for zz in range(Z):
+            va = D.at[zz, x, y, :, A]
+            va[...] = (va[...].astype(F32) + ra1[j, 1, zz].astype(F32) + ra2[j, zz].astype(F32)).astype(BF)
+        for k in range(nz):
+            rc(j, 4 + nz + k, D.at[zi[k], x, y, :, A], ra3.at[j, k], zs[k])
+        for k in range(nz):
+            got(j, 4 + k, rc2.at[j, k])
+        for yy in range(2):
+            va = D.at[z, x, yy, :, C]
+            t = va[...].astype(F32)
+            for k in range(nz):
+                t = t + rc2[j, k, yy].astype(F32)
+            va[...] = t.astype(BF)
+        rc(j, 4 + 2 * nz, D.at[z, x, 1 - y, :, C], rc3.at[j], yp)
+    pcopies = {}
+    def lay(ref, val, first, stride, n):
+        for t in range(nt):
+            ref[pl.ds(first + t, n, stride=stride), :] = val[:, 128 * t:128 * t + 128]
+    def stage4(j):
+        D = part.at[j % nb]
+        for k in range(nz):
+            got(j, 4 + nz + k, ra3.at[j, k])
+        got(j, 4 + 2 * nz, rc3.at[j])
+        a = D[z, x, y, :, 0:lanes_a].astype(F32)
+        for k in range(nz):
+            a = a + ra3[j, k].astype(F32)
+        b = D[z, x, y, :, lanes_a:wide].astype(F32) + rc3[j].astype(F32)
+        v = jnp.concatenate([a, b], 1)
+        if j in (0, 1):
+            lay(fc2_o, v, j * rows * nt, nt, rows)
+        elif j == 6:
+            lay(skip_o, v, 0, nt, rows)
+        else:
+            lo = v[0:half]; hi = v[half:rows]
+            keep[j - 2, 0:half, :] = jnp.where(c == 0, lo, hi)
+            give[j - 2, 0:half, :] = jnp.where(c == 0, hi, lo)
+            cp = pltpu.make_async_remote_copy(give.at[j - 2], take.at[j - 2], psend.at[j - 2], precv.at[j - 2], device_id=pp, device_id_type=MESH)
+            cp.start(); pcopies[j] = cp
+    def stage5(j):
+        pcopies[j].wait_recv()
+        mine = keep[j - 2, 0:half, :]; theirs = take[j - 2, 0:half, :]
+        first = jnp.where(c == 0, mine, theirs); second = jnp.where(c == 0, theirs, mine)
+        if j in (2, 3):
+            lay(fc1_o, first, nt * 2 * (j - 2), 4 * nt, half)
+            lay(fc1_o, second, nt * (2 * (j - 2) + 1), 4 * nt, half)
+        elif j == 5:
+            lay(qkv_o, first, 0, 3 * nt, half)
+            lay(qkv_o, second, nt, 3 * nt, half)
+        else:
+            lay(qkv_o, first, 2 * nt, 3 * nt, half)
+            lay(proj_o, second, 0, nt, half)
+    def vec_first():
+        s = vec_ref[dp]
+        for k in range(len(dps)):
+            pltpu.make_async_remote_copy(vgot.at[k], vgot.at[k], vsend.at[k], vrecv.at[k], device_id=pp, device_id_type=MESH).wait_recv()
+            s = s + vgot[k]
+        vall[f] = s
+        for k, d in enumerate(fs):
+            cp = pltpu.make_async_remote_copy(vall.at[f], vall.at[f], wsend.at[k], wrecv.at[k], device_id=d, device_id_type=MESH)
+            cp.start(); vcopies.append(cp)
+    def vec_last():
+        for k in range(3):
+            src = lax.rem(f - (k + 1) + 4, 4)
+            pltpu.make_async_remote_copy(vall.at[src], vall.at[src], wsend.at[k], wrecv.at[k], device_id=pp, device_id_type=MESH).wait_recv()
+        vec_o[...] = vall[0] + vall[1] + vall[2] + vall[3]
+    for j in range(7 + 4):
+        if j < 7: stage1(j)
+        if j == 1: vec_first()
+        if j == 2: vec_last()
+        if 0 <= j - 1 < 7: stage2(j - 1)
+        if 0 <= j - 2 < 7: stage3(j - 2)
+        if 0 <= j - 3 < 7: stage4(j - 3)
+        if 2 <= j - 4 < 6: stage5(j - 4)
+    for j in range(max(0, 7 - nb), 7):
+        for cp in started[j]: cp.wait_send()
+    for cp in pcopies.values(): cp.wait_send()
+    for cp in vcopies: cp.wait_send()
+    for a, b in copies.values(): b.wait_send()
+
+def scatter(acts, vec_grad, dpn, wide):
+    Z = dpn // 2; length = acts[0].shape[0]
+    rows = 2 * wide // (4 * dpn)
+    lanes_a = (wide // 128 * 2 + 1) // 3 * 128
+    lc = wide - lanes_a
+    hbm = pl.BlockSpec(memory_space=pl.ANY); vm = pl.BlockSpec(memory_space=pltpu.VMEM)
+    D = pltpu.SemaphoreType.DMA
+    half = rows // 2; hp = -(-half // 8) * 8
+    nv = vec_grad.shape[0] // dpn
+    nz = Z - 1; ns = 5 + 2 * nz
+    nb = 4
+    V = pltpu.VMEM
+    outs = [rows * wide // 128, 3 * half * wide // 128, half * wide // 128, 4 * half * wide // 128, 2 * rows * wide // 128]
+    res = pl.pallas_call(
+        functools.partial(scatter_kernel, Z, wide, rows, lanes_a, length),
+        out_shape=tuple(jax.ShapeDtypeStruct((n, 128), F32) for n in outs) + (jax.ShapeDtypeStruct((1, nv), F32),),
+        in_specs=[hbm] * 10 + [vm], out_specs=(vm,) * 6,
+        scratch_shapes=[V((6, 2 * length, wide), BF), V((6, 2 * length, wide), BF), V((nb, Z, 2, 2, rows, wide), BF),
+                        V((7, 2, Z, rows, lanes_a), BF), V((7, Z, rows, lanes_a), BF), V((7, nz, rows, lanes_a), BF),
+                        V((7, Z, 2, rows, lc), BF), V((7, nz, 2, rows, lc), BF), V((7, rows, lc), BF),
+                        V((4, hp, wide), F32), V((4, hp, wide), F32), V((4, hp, wide), F32),
+                        V((dpn - 1, 1, nv), F32), V((4, 1, nv), F32),
+                        D((12,)), D((12,)), D((12,)), D((7, ns)), D((7, ns)), D((4,)), D((4,)), D((dpn - 1,)), D((dpn - 1,)), D((3,)), D((3,))],
+        compiler_params=pltpu.CompilerParams(collective_id=1, has_side_effects=True, vmem_limit_bytes=62 << 20),
+        name="scatter",
+    )(*acts, vec_grad.reshape(dpn, 1, nv))
+    return tuple(r.reshape(-1) for r in res)
+
+
+def whole_rows(width, dp, fsdp, items):
+    return fsdp == 4 and dp % 2 == 0 and width % (dp * 16) == 0 and items == 1
+
+
+def pad_rows(value, rows):
+    return jnp.pad(value, ((0, rows - value.shape[0]), (0, 0)))
+
+
+def by_unit(value, units, chips):
+    rows, wide = value.shape
+    return value.reshape(rows, chips, units, -1).transpose(0, 2, 1, 3).reshape(rows, wide)
+
+
+def fast_body(block_in, skip_in, out_grad, caption_len, skip_w, qkv_w, proj_w, fc1_w, fc2_w, vectors):
+    items, length, width = block_in.shape
+    heads = HEADS
+    head_dim = width // heads
+    hidden = FF
+    scale = head_dim ** (-0.5)
+    dpn = lax.axis_size("dp")
+    chips = 2 * dpn
+    rows = -(-length // 16) * 16
+    skip_u, qp_u, fc1_u, fc2_u, vec = gather(skip_w, qkv_w, proj_w, fc1_w, fc2_w, vectors, dpn, width)
+    skip_m = skip_u.reshape(2 * width, width)
+    qp_m = qp_u.reshape(4, width, width)
+    fc1_m = fc1_u.reshape(hidden // width, width, width)
+    fc2_m = fc2_u.reshape(hidden, width)
+    vec = vec.reshape(-1)
+    gain_one = vec[0:width]
+    shift_one = vec[width : 2 * width]
+    gain_two = vec[2 * width : 3 * width]
+    shift_two = vec[3 * width : 4 * width]
+    skip_bias = vec[4 * width : 5 * width]
+    proj_bias = vec[5 * width : 6 * width]
+    fc2_bias = vec[6 * width : 7 * width]
+    fc1_bias = vec[7 * width :]
+    place = lax.broadcasted_iota(jnp.int32, (1, rows), 1)
+    valid = ((place < 1 + caption_len[:, None]) | (place >= 1 + CAPTION)) & (place < length)
+    joined = pad_rows(jnp.concatenate([block_in[0], skip_in[0]], -1).astype(jnp.bfloat16), rows)
+    first = product(joined, skip_m) + skip_bias
+    normed_one = norm_rows(first, gain_one, shift_one).astype(jnp.bfloat16)
+    query, keys, values = (
+        product(normed_one, qp_m[i]).astype(jnp.bfloat16).reshape(items, rows, heads, head_dim)
+        for i in range(3)
+    )
+    scores = attention_scores(query, keys, valid, scale)
+    top = jnp.max(scores, -1, keepdims=True)
+    expd = jnp.exp(scores - top)
+    total = jnp.sum(expd, -1, keepdims=True)
+    probs = expd / total
+    log_total = top + jnp.log(total)
+    mixed = (
+        jnp.einsum("ihst,ithd->ishd", probs.astype(jnp.bfloat16), values, preferred_element_type=jnp.float32)
+        .astype(jnp.bfloat16)
+        .reshape(rows, width)
+    )
+    second = first + (product(mixed, qp_m[3]) + proj_bias)
+    normed_two = norm_rows(second, gain_two, shift_two).astype(jnp.bfloat16)
+    inner = (
+        jnp.concatenate([product(normed_two, fc1_m[i]) for i in range(hidden // width)], 1) + fc1_bias
+    )
+    active = gelu_exact(inner).astype(jnp.bfloat16)
+    block_out = second + (product(active, fc2_m) + fc2_bias)
+    grad_out = pad_rows(out_grad[0], rows)
+    grad_mlp = grad_out.astype(jnp.bfloat16)
+    d_fc2_bias = column_sum(grad_mlp)
+    d_active = right_product(grad_mlp, fc2_m)
+    gelu_value, gelu_pull = jax.vjp(gelu_exact, inner)
+    grad_inner = gelu_pull(d_active)[0].astype(jnp.bfloat16)
+    d_fc1_bias = column_sum(grad_inner)
+    d_normed_two = sum(
+        right_product(grad_inner[:, width * i : width * (i + 1)], fc1_m[i])
+        for i in range(hidden // width)
+    )
+    norm_value_two, norm_pull_two = jax.vjp(norm_rows, second, gain_two, shift_two)
+    d_second_norm, d_gain_two, d_shift_two = norm_pull_two(d_normed_two)
+    grad_second = grad_out + d_second_norm
+    grad_attn = grad_second.astype(jnp.bfloat16)
+    d_proj_bias = column_sum(grad_attn)
+    grad_mixed = (
+        right_product(grad_attn, qp_m[3]).astype(jnp.bfloat16).reshape(items, rows, heads, head_dim)
+    )
+    again_scores = attention_scores(query, keys, valid, scale)
+    again_probs = jnp.exp(again_scores - log_total)
+    d_probs = jnp.einsum("ishd,ithd->ihst", grad_mixed, values, preferred_element_type=jnp.float32)
+    inner_sum = jnp.sum(again_probs * d_probs, -1, keepdims=True)
+    grad_scores = (again_probs * (d_probs - inner_sum)).astype(jnp.bfloat16)
+    d_query = jnp.einsum("ihst,ithd->ishd", grad_scores, keys, preferred_element_type=jnp.float32) * scale
+    d_keys = jnp.einsum("ihst,ishd->ithd", grad_scores, query, preferred_element_type=jnp.float32) * scale
+    d_values = jnp.einsum(
+        "ihst,ishd->ithd", again_probs.astype(jnp.bfloat16), grad_mixed, preferred_element_type=jnp.float32
+    )
+    grad_triple = jnp.concatenate(
+        [t.reshape(rows, width).astype(jnp.bfloat16) for t in (d_query, d_keys, d_values)], 1
+    )
+    d_normed_one = sum(
+        right_product(grad_triple[:, width * i : width * (i + 1)], qp_m[i]) for i in range(3)
+    )
+    norm_value_one, norm_pull_one = jax.vjp(norm_rows, first, gain_one, shift_one)
+    d_first_norm, d_gain_one, d_shift_one = norm_pull_one(d_normed_one)
+    grad_first = (grad_second + d_first_norm).astype(jnp.bfloat16)
+    d_skip_bias = column_sum(grad_first)
+    in_grad = right_product(grad_first[:length], skip_m[:width])
+    skip_grad = right_product(grad_first[:length], skip_m[width:])
+    vec_grad = jnp.concatenate(
+        [d_gain_one, d_shift_one, d_gain_two, d_shift_two, d_skip_bias, d_proj_bias, d_fc2_bias, d_fc1_bias]
+    )
+    pieces = scatter(
+        (
+            by_unit(active, hidden // width, chips),
+            grad_mlp,
+            normed_two,
+            grad_inner,
+            mixed,
+            grad_attn,
+            normed_one,
+            grad_triple,
+            by_unit(joined, 2, chips),
+            grad_first,
+        ),
+        vec_grad,
+        dpn,
+        width,
+    )
+    shape = block_in.shape
+    return (block_out[:length].reshape(shape), in_grad.reshape(shape), skip_grad.reshape(shape)) + pieces
+
+
 def body(block_in, skip_in, out_grad, caption_len, skip_w, qkv_w, proj_w, fc1_w, fc2_w, vectors):
     items, length, width = block_in.shape
+    if whole_rows(width, lax.axis_size("dp"), lax.axis_size("fsdp"), items):
+        return fast_body(
+            block_in, skip_in, out_grad, caption_len, skip_w, qkv_w, proj_w, fc1_w, fc2_w, vectors
+        )
     heads = HEADS
     head_dim = width // heads
     hidden = FF
     rows = items * length
     scale = head_dim ** (-0.5)
-    owners = lax.axis_size(("dp", "fsdp"))
-    if whole_rows(width, lax.axis_size("dp"), lax.axis_size("fsdp")):
-        skip_u, qp_u, fc1_u, fc2_u, vec = gather(
-            skip_w, qkv_w, proj_w, fc1_w, fc2_w, vectors, lax.axis_size("dp"), width
-        )
-        skip_m = skip_u.reshape(2 * width, width)
-        qp_u = qp_u.reshape(4, width, width)
-        qkv_m = jnp.concatenate([qp_u[0], qp_u[1], qp_u[2]], 1)
-        proj_m = qp_u[3]
-        fc1_m = jnp.concatenate([t.reshape(width, width) for t in fc1_u], 1)
-        fc2_m = fc2_u.reshape(hidden, width)
-        vec = vec.reshape(-1)
-    else:
-        gathered = tuple(
-            lax.all_gather(w.astype(jnp.bfloat16), ("dp", "fsdp"), axis=0, tiled=True)
-            for w in (skip_w, qkv_w, proj_w, fc1_w, fc2_w)
-        )
-        skip_m, qkv_m, proj_m, fc1_m, fc2_m = unpack(gathered, width, hidden)
-        vec = lax.all_gather(vectors, "dp", axis=0, tiled=True)
+    gathered = (
+        lax.all_gather(skip_w.astype(jnp.bfloat16), ("dp", "fsdp"), axis=0, tiled=True),
+        lax.all_gather(qkv_w.astype(jnp.bfloat16), ("dp", "fsdp"), axis=0, tiled=True),
+        lax.all_gather(proj_w.astype(jnp.bfloat16), ("dp", "fsdp"), axis=0, tiled=True),
+        lax.all_gather(fc1_w.astype(jnp.bfloat16), ("dp", "fsdp"), axis=0, tiled=True),
+        lax.all_gather(fc2_w.astype(jnp.bfloat16), ("dp", "fsdp"), axis=0, tiled=True),
+    )
+    skip_m, qkv_m, proj_m, fc1_m, fc2_m = unpack(gathered, width, hidden)
+    vec = lax.all_gather(vectors, "dp", axis=0, tiled=True)
     gain_one = vec[0:width]
     shift_one = vec[width : 2 * width]
     gain_two = vec[2 * width : 3 * width]
@@ -286,6 +622,14 @@
     inner = product(normed_two, fc1_m) + fc1_bias
     active = gelu_exact(inner).astype(jnp.bfloat16)
     block_out = second + (product(active, fc2_m) + fc2_bias)
+    again = (
+        lax.all_gather(skip_w.astype(jnp.bfloat16), ("dp", "fsdp"), axis=0, tiled=True),
+        lax.all_gather(qkv_w.astype(jnp.bfloat16), ("dp", "fsdp"), axis=0, tiled=True),
+        lax.all_gather(proj_w.astype(jnp.bfloat16), ("dp", "fsdp"), axis=0, tiled=True),
+        lax.all_gather(fc1_w.astype(jnp.bfloat16), ("dp", "fsdp"), axis=0, tiled=True),
+        lax.all_gather(fc2_w.astype(jnp.bfloat16), ("dp", "fsdp"), axis=0, tiled=True),
+    )
+    skip_m, qkv_m, proj_m, fc1_m, fc2_m = unpack(again, width, hidden)
     grad_out = out_grad.reshape(rows, width)
     grad_mlp = grad_out.astype(jnp.bfloat16)
     d_fc2_bias = column_sum(grad_mlp)
@@ -333,6 +677,7 @@
     grad_joined = right_product(grad_first, skip_m).reshape(items, length, 2 * width)
     in_grad = grad_joined[:, :, 0:width]
     skip_grad = grad_joined[:, :, width:]
+    owners = lax.axis_size(("dp", "fsdp"))
     pairs = (
         (joined, grad_first),
         (normed_one, grad_triple),

time: 1570 us -> 581 us (0.37)
  waiting for transfers between devices: 985 us -> 0 us
  Pallas kernels: 166 us -> 347 us
  local copies, waits for them, and re-layouts: 197 us -> 91.7 us
  blocking collectives: 49.1 us -> 0 us
  matrix products: 139 us -> 94.2 us
  other arithmetic: 13.2 us -> 37.1 us
    unnamed x2 -> x0, waiting for transfers between devices: 985 us -> none
    pallas_call x0 -> x1, Pallas kernels: none -> 181 us  [scatter(): pl.pallas_call(functools.partial(scatter_kernel, Z, wide, rows, lanes_a,...]
    another operation x6 -> x0, local copies, waits for them, and re-layouts: 89.1 us -> none  [the longest x5 79.4 us: body(): flat_piece(pair[0], pair[1])]
    unnamed x1 -> x0, blocking collectives: 42.1 us -> none
    dot_general x10 -> x5, matrix products: 55.1 us -> 18.2 us  [the longest x1 5.46 us: fast_body(): jnp.einsum('ishd,ithd->ihst', grad_mixed, values, preferred_element_type=...]
    unnamed x141 -> x168, local copies, waits for them, and re-layouts: 68.7 us -> 39.3 us
    transpose x0 -> x1, other arithmetic: none -> 18.9 us  [by_unit(): value.reshape(rows, chips, units, -1).transpose(0, 2, 1, 3)]
    dot_general x5 -> x10, matrix products: 46.2 us -> 33.3 us  [product(): return jnp.dot(left, right, preferred_element_type=jnp.float32)]
  transfers between devices with their start and end apart: 1 -> 0, of which waited for: 1 -> 0; matrix products, arithmetic and copies ran while one was open for 1% -> 0% of each run, Pallas kernels for 0% -> 0%
where the time goes in v2:
time: 581 us; the launch traced here: 572 us
  Pallas kernels  347 us (60%)
  matrix products  94.2 us (16%)
  local copies, waits for them, and re-layouts  91.7 us (16%)
  other arithmetic  37.1 us (6%)
    pallas_call x1, Pallas kernels, scatter(): pl.pallas_call(functools.partial(scatter_kernel, Z, wide, rows, lanes_a,...  181 us
    pallas_call x1, Pallas kernels, gather(): pl.pallas_call(functools.partial(gather_kernel, Z, wide, rows, lanes_a),...  166 us
    dot_general x11, matrix products, right_product(): lax.dot_general(left, right, (((1,), (1,)), ((), ())), preferred_element_...  40.4 us
    unnamed x168, local copies, waits for them, and re-layouts  39.3 us
    dot_general x10, matrix products, product(): return jnp.dot(left, right, preferred_element_type=jnp.float32)  33.3 us
    transpose x1, other arithmetic, by_unit(): value.reshape(rows, chips, units, -1).transpose(0, 2, 1, 3)  18.9 us

profile of v2, /device:TPU:0, one launch (start us, length us, event | category | flops | bytes accessed | tf_op | source)
XLA Modules:
  0.0 572.2 jit_solution(800712099647493855)
XLA Ops:
  6.5 165.9 %gather.1 = (bf16[4,2,2,2,72,1152]{5,4,3,2,1,0:T(8,128)(2,1)S(1)}, bf16[4,4,2,2,72,1152]{5,4,3,2,1,0:T(8,128)(2,1)S(1)}, bf16[4,4,2,2,72,1152]{5,4,3,2,1,0:T(8,1...) custom-call(f32[648,128]{1,0:T(8,128)S(1)} %bitcast.123, f32[972,128]{1,0:T(8,128)S(1)} %bitcast.122, ...), custom_call_target="tpu_custom_call" | custom-call | tf_op jit(solution)/shard_map/gather/pallas_call | solution.py:207
  172.4 4.0 copy-done
  176.4 2.4 copy-done.1
  179.6 2.0 copy.46
  181.7 3.8 copy.45
  185.6 5.2 fusion.57
  192.0 1.9 convert_reduce_fusion.1
  193.9 10.0 %fusion.53 = (bf16[1,4,2,2,72,1152]{5,4,3,2,1,0:T(8,128)(2,1)}, bf16[1,4,2,2,72,1152]{5,4,3,2,1,0:T(8,128)(2,1)}, bf16[1,4,2,2,72,1152]{5,4,3,2,1,0:T(8,128)(2,1...) fusion(bf16[4,4,2,2,72,1152]{5,4,3,2,1,0:T(8,128)(2,1)} %get-tu, ...), kind=kLoop, calls=%fused_computation.134 | loop fusion | bytes 42467328 | tf_op jit(solution)/shard_map/slice | solution.py:497
  203.9 3.0 convolution_convert_fusion.1
  207.9 3.4 convolution_convert_fusion.2
  213.3 2.2 fusion.58
  216.7 2.5 copy-done.7
  221.4 5.3 fusion.33
  227.7 1.4 fusion.59
  232.5 2.5 fusion.61
  235.0 2.5 fusion.62
  237.4 2.4 fusion.63
  239.9 22.3 %convert_reduce_fusion = (f32[4608]{0:T(1024)S(1)}, bf16[336,4608]{1,0:T(8,128)(2,1)S(1)}, f32[336,4608]{1,0:T(8,128)}) fusion(f32[4608]{0:T(1024)S(1)} %slice.134, f32[336,1152]{1,0:T(8,128)} %fusion.63, f32[336,1152]{1,0:T(8,128)} %fusion.62, f32[336,1152]{1,0:T(8,128)} %fusion.61, f32[336,1152]{1,0:T(8,128)S(1)} %fusion.60, ...), kind=kOutput, calls=%fused_computation.31 | convolution fusion | flops 3688017408 | bytes 26910720 | tf_op jit(solution)/shard_map/dot_general | solution.py:45
  262.2 4.2 fusion.37
  269.0 1.6 multiply_reduce_fusion.1
  274.5 1.5 copy.51
  276.1 5.1 fusion.30
  281.3 5.5 multiply_reduce_fusion
  287.0 1.7 multiply_convert_fusion
  292.5 1.4 fusion.64
  296.1 2.9 multiply_reduce_fusion.2
  299.2 2.4 fusion.51
  301.6 3.1 convert_reduce_fusion.3
  305.5 1.5 copy.62
  306.9 2.2 copy.61
  309.2 2.6 copy.60
  311.8 2.9 pad_maximum_fusion.t_ref
  314.7 2.7 copy.55
  317.4 2.8 copy.56
  320.2 2.8 copy.57
  323.0 2.7 copy.58
  325.8 18.9 %fusion.24 = bf16[336,4,16,72]{0,3,1,2:T(8,128)(2,1)S(1)} fusion(f32[16,4,72]{2,1,0:T(4,128)S(1)} %slice.143, f32[336,4,4,72]{0,3,2,1:T(8,128)} %bitcast.146, f32[336,4,4,72]{0,3,2,1:T(8,128)} %bitcast.145, f32[336,4,4,72]{0,3,2,1:T(8,128)} %bitcast.144, f32[336,4,4,72]{0,3,2,1:T(8,128)} %bitcast.143), kind=kLoop, calls=%fused_computation.53 | loop fusion | flops 106831872 | bytes 9308160 | tf_op jit(solution)/shard_map/transpose | solution.py:448
  344.7 2.1 copy.59
  346.8 5.7 copy.64.z_ref
  352.5 2.2 copy.65.o_ref
  354.7 1.4 fusion.28
  357.5 3.8 copy.66.j_ref
  361.3 180.9 %scatter.1 = (f32[648,128]{1,0:T(8,128)}, f32[972,128]{1,0:T(8,128)}, f32[324,128]{1,0:T(8,128)}, f32[1296,128]{1,0:T(8,128)}, f32[1296,128]{1,0:T(8,128)}, /*index=5*/f32[1,1584]{1,0:T(1,128)}) custom-call(bf16[336,4608]{1,0:T(8,128)(2,1)} %copy.64.z_ref, bf16[336,1152]{1,0:T(8,128)(2,1)} %get-tuple-element.59.gm_ref, bf16[336,1152]{1,0:T(8,128)(2,1)} %copy-done.34, ...), custom_call_target="tpu_custom_call" | custom-call | tf_op jit(solution)/shard_map/scatter/pallas_call | solution.py:422
  543.5 3.0 fusion.55
  547.9 2.7 copy.69
  552.0 2.7 copy.68
  554.7 10.3 %fusion.25 = f32[336,1152]{1,0:T(8,128)S(1)} fusion(bf16[4608,1152]{1,0:T(8,128)(2,1)} %bitcast.181, f32[336,4608]{1,0:T(8,128)} %get-tuple-element.57, f32[336,1152]{1,0:T(8,128)S(1)} %copy-done.46, f32[336,1152]{1,0:T(8,128)S(1)} %copy-done.45, f32[336,1152]{1,0:T(8,128)S(1)} %copy-done.44, f32[336,1152]{1,0:T(8,128)S(1)} %copy-done.43, f32[4608]{0:T(1024)S(1)} %slice.134), kind=kOutput, calls=%fused_computation.54 | convolution fusion | flops 3578093568 | bytes 24569856 | tf_op jit(solution)/shard_map/dot_general | solution.py:35
  565.3 2.7 copy.67
  (204 shorter events, 40.9 us)
Async XLA Ops:
  6.5 173.2 %copy-start.47 = (f32[1,334,1152]{2,0,1:T(1,128)S(1)}, f32[1,334,1152]{2,0,1:T(1,128)}, u32[]{:S(2)}) copy-start(f32[1,334,1152]{2,0,1:T(1,128)} %param.11) | copy-start | bytes 4617220
  172.4 4.0 copy-start
  178.9 6.6 %copy-start.53 = (f32[8,1584]{1,0:T(8,128)}, f32[8,1584]{1,0:T(8,128)S(1)}, u32[]{:S(2)}) copy-start(f32[8,1584]{1,0:T(8,128)S(1)} %reduce.6) | copy-start | bytes 152068
  179.6 12.1 %copy-start.57 = (f32[1152]{0:T(1024)}, f32[1152]{0:T(1024)S(1)}, u32[]{:S(2)}) copy-start(f32[1152]{0:T(1024)S(1)} %get-tuple-element.83) | copy-start | bytes 13828
  181.6 9.1 %copy-start.21 = (bf16[1,334,1152]{1,2,0:T(8,128)(2,1)}, bf16[1,334,1152]{1,2,0:T(8,128)(2,1)S(1)}, u32[]{:S(2)}) copy-start(bf16[1,334,1152]{1,2,0:T(8,128)(2,1)S(1)} %copy.46) | copy-start | bytes 2308612
  185.5 5.3 copy-start.23
  185.5 5.6 copy-start.48
  185.5 8.4 %slice-start = ((s8[10616832]{0:T(1024)(128)(4,1)}), s8[4194304]{0:T(1024)(128)(4,1)S(1)}, s32[]{:S(2)}) async-start(s8[10616832]{0:T(1024)(128)(4,1)} %bitcast.117), calls=%async_computation | async-start | bytes 8388608
  185.5 8.4 %slice-start.1 = ((s8[10616832]{0:T(1024)(128)(4,1)}), s8[4194304]{0:T(1024)(128)(4,1)S(1)}, s32[]{:S(2)}) async-start(s8[10616832]{0:T(1024)(128)(4,1)} %bitcast.117), calls=%async_computation.1 | async-start | bytes 8388608
  190.8 3.1 copy-start.61
  190.8 3.1 slice-start.2
  191.1 2.8 copy-start.65
  193.9 25.3 %copy-start.31 = (bf16[336,1152]{1,0:T(8,128)(2,1)}, bf16[336,1152]{1,0:T(8,128)(2,1)S(1)}, u32[]{:S(2)}) copy-start(bf16[336,1152]{1,0:T(8,128)(2,1)S(1)} %get-tuple-element.99.n_ref) | copy-start | bytes 2322436
  207.9 5.4 copy-start.16
  212.6 2.9 copy-start.18
  215.5 3.7 copy-start.7
  215.5 3.7 copy-start.14
  221.4 5.4 copy-start.26
  221.4 6.3 %copy-start.9 = (f32[336,1152]{1,0:T(8,128)S(1)}, f32[336,1152]{1,0:T(8,128)}, u32[]{:S(2)}) copy-start(f32[336,1152]{1,0:T(8,128)} %copy-done.8) | copy-start | bytes 4644868
  221.4 6.3 %copy-start.37 = (bf16[1,4,2,2,72,1152]{5,4,3,2,1,0:T(8,128)(2,1)S(1)}, bf16[1,4,2,2,72,1152]{5,4,3,2,1,0:T(8,128)(2,1)}, u32[]{:S(2)}) copy-start(bf16[1,4,2,2,72,1152]{5,4,3,2,1,0:T(8,128)(2,1)} %get-tuple-element.98) | copy-start | bytes 7962628
  221.4 6.3 %copy-start.69 = (f32[1152]{0:T(1024)S(1)}, f32[1152]{0:T(1024)}, u32[]{:S(2)}) copy-start(f32[1152]{0:T(1024)} %get-tuple-element.81) | copy-start | bytes 13828
  229.8 7.6 %copy-start.34 = (bf16[336,1152]{1,0:T(8,128)(2,1)}, bf16[336,1152]{1,0:T(8,128)(2,1)S(1)}, u32[]{:S(2)}) copy-start(bf16[336,1152]{1,0:T(8,128)(2,1)S(1)} %add_convert_fusion.2.m_ref) | copy-start | bytes 2322436
  232.5 7.4 %copy-start.42 = (f32[336,1152]{1,0:T(8,128)}, f32[336,1152]{1,0:T(8,128)S(1)}, u32[]{:S(2)}) copy-start(f32[336,1152]{1,0:T(8,128)S(1)} %fusion.60) | copy-start | bytes 4644868
  262.2 6.8 %copy-start.28 = (bf16[336,4608]{1,0:T(8,128)(2,1)}, bf16[336,4608]{1,0:T(8,128)(2,1)S(1)}, u32[]{:S(2)}) copy-start(bf16[336,4608]{1,0:T(8,128)(2,1)S(1)} %get-tuple-element.56.gu_ref) | copy-start | bytes 9289732
  273.2 2.9 copy-start.60
  276.1 5.2 copy-start.20
  276.1 5.2 copy-start.27
  281.2 5.5 slice-start.3
  281.3 5.8 %slice-start.4 = ((s8[8257536]{0:T(1024)(128)(4,1)}), s8[4063232]{0:T(1024)(128)(4,1)S(1)}, s32[]{:S(2)}) async-start(s8[8257536]{0:T(1024)(128)(4,1)} %bitcast.125), calls=%async_computation.4 | async-start | bytes 8126464
  290.1 3.8 copy-start.24
  291.1 4.2 copy-start.25
  291.2 2.7 copy-start.35
  296.1 3.0 copy-start.68
  301.5 3.2 copy-start.64
  306.9 4.9 copy-start.29
  320.2 5.5 copy-start.54
  346.8 7.9 %copy-start.22 = (bf16[1,334,1152]{1,2,0:T(8,128)(2,1)S(1)}, bf16[1,334,1152]{1,2,0:T(8,128)(2,1)}, u32[]{:S(2)}) copy-start(bf16[1,334,1152]{1,2,0:T(8,128)(2,1)} %copy-done.21) | copy-start | bytes 2308612
  543.5 3.0 copy-start.33
  550.6 4.1 copy-start.43
  550.6 4.1 copy-start.44
  550.6 4.1 copy-start.45
  550.6 4.1 copy-start.46
  554.7 10.3 %copy-start.63 = (f32[1152]{0:T(1024)S(1)}, f32[1152]{0:T(1024)}, u32[]{:S(2)}) copy-start(f32[1152]{0:T(1024)} %get-tuple-element.78) | copy-start | bytes 13828
  565.0 3.0 copy-start.55
  565.0 3.8 copy-start.52
  565.0 4.6 copy-start.56
  565.3 5.0 copy-start.51
  565.3 5.9 %copy-start.50 = (f32[1296,128]{1,0:T(8,128)S(1)}, f32[1296,128]{1,0:T(8,128)}, u32[]{:S(2)}) copy-start(f32[1296,128]{1,0:T(8,128)} %get-tuple-element.29) | copy-start | bytes 1990660
  (27 other events, 45.8 us)

commit v3 on v0

--- a/solution.py
+++ b/solution.py
@@ -1,6 +1,10 @@
+import functools
+
 import jax
 import jax.numpy as jnp
 from jax import lax
+from jax.experimental import pallas as pl
+from jax.experimental.pallas import tpu as pltpu
 from jax.sharding import PartitionSpec as P
 
 HEADS = 16
@@ -67,8 +71,818 @@
     return grad_rows
 
 
+MESH = pl.DeviceIdType.MESH
+BF=jnp.bfloat16; F32=jnp.float32
+SPLIT = 384
+
+
+def unit_lanes(value, units, chips):
+    seg = value.shape[1] // (units * chips)
+    return [
+        jnp.concatenate([value[:, (s * units + u) * seg : (s * units + u + 1) * seg] for s in range(chips)], 1)
+        for u in range(units)
+    ]
+
+
+def row_loop(total, step, fn):
+    def one(n, carry):
+        fn(pl.ds(pl.multiple_of(n * step, step), step))
+        return carry
+    lax.fori_loop(0, total // step, one, 0)
+
+
+def forward_kernel(Z, wide, rows, lanes_a, length, padded,
+                   cap_ref, skip_ref, qkv_ref, proj_ref, fc1_ref, fc2_ref, vec_ref, in_ref, sk_ref, og_ref,
+                   skip_o, qp_o, fc1_o, fc2_o, vec_o, out_o, j_o, h0_o, a_o, t_o, mix_o, h1_o, m_o, z_o, gm_o, gu_o,
+                   own, mine, give, take, vbuf, vecs, b1s, xin, gin, jn, jp, h0, a, t, oacc, mix, h1, m, zz, der, gm, gu, tmp, acc, wbuf,
+                   send, recv, lsem, psend, precv, vsend, vrecv, isem, osem, wsem):
+    dp = lax.axis_index("dp"); f = lax.axis_index("fsdp")
+    z = dp // 2; x = dp % 2; y = f // 2; c = f % 2
+    nt = wide // 128
+    half = rows // 2
+    chips = 4 * Z
+    A = pl.ds(0, lanes_a); C = pl.ds(lanes_a, wide - lanes_a)
+    zs = [(lax.rem(z + k, Z) * 2 + x, f) for k in range(1, Z)]
+    xp = (z * 2 + 1 - x, f)
+    yp = (dp, (1 - y) * 2 + c)
+    pp = (dp, y * 2 + 1 - c)
+    ndp = 2 * Z
+    others = [(lax.rem(dp + k, ndp), f) for k in range(1, ndp)]
+    bar = pltpu.get_barrier_semaphore()
+    for d in others + [yp, pp]:
+        pl.semaphore_signal(bar, inc=1, device_id=d, device_id_type=MESH)
+    loads = [
+        pltpu.make_async_copy(in_ref, xin.at[0], isem.at[0]),
+        pltpu.make_async_copy(sk_ref, xin.at[1], isem.at[1]),
+        pltpu.make_async_copy(og_ref, gin, isem.at[2]),
+    ]
+    for cp in loads: cp.start()
+    for j in range(nt):
+        own[0, :, 128 * j:128 * j + 128] = skip_ref[pl.ds(j, rows, stride=nt), :].astype(BF)
+    pl.semaphore_wait(bar, len(others) + 2)
+
+    nz = Z - 1
+    waits = []
+    def rc(i, slot, src, dst, dev):
+        cp = pltpu.make_async_remote_copy(src, dst, send.at[i, slot], recv.at[i, slot], device_id=dev, device_id_type=MESH)
+        cp.start(); waits.append(cp)
+    def got(i, slot, dst):
+        pltpu.make_async_remote_copy(dst, dst, send.at[i, slot], recv.at[i, slot], device_id=pp, device_id_type=MESH).wait_recv()
+    def unit(i, cc):
+        if i == 0: return skip_o.at[:, :, :, cc]
+        if i in (1, 2): return qp_o.at[2 * (i - 1) + cc]
+        if i in (3, 4): return fc1_o.at[2 * (i - 3) + cc]
+        return fc2_o.at[2 * cc + (i - 5)]
+    pc = {}
+    lc = {}
+    def stage1(i):
+        U = unit(i, c)
+        if i in (1, 2, 3, 4):
+            pc[i].wait_recv()
+            p = mine[i - 1, 0:half, :]
+            q = take[i - 1, :, :].astype(F32)[0:half]
+            lo = jnp.where(c == 0, p, q); hi = jnp.where(c == 0, q, p)
+            own[i, :, :] = jnp.concatenate([lo, hi], 0).astype(BF)
+        lc[i] = pltpu.make_async_copy(own.at[i], U.at[z, x, y], lsem.at[i]); lc[i].start()
+        rc(i, 2 * nz, own.at[i, :, C], U.at[z, x, y, :, C], yp)
+        for k in range(1, Z):
+            rc(i, k - 1, own.at[i, :, A], U.at[z, x, y, :, A], zs[k - 1])
+    def stage2(i):
+        U = unit(i, c)
+        lc[i].wait()
+        got(i, 2 * nz, U.at[z, x, 1 - y, :, C])
+        for k in range(1, Z):
+            rc(i, nz + k - 1, U.at[z, x, :, :, C], U.at[z, x, :, :, C], zs[k - 1])
+        for k in range(1, Z):
+            got(i, k - 1, U.at[lax.rem(z - k + Z, Z), x, y, :, A])
+        L = U.at[:, x, y, :, A]
+        rc(i, 2 * nz + 1, L, L, xp)
+        rc(i, 2 * nz + 2, L, L, yp)
+        rc(i, 2 * nz + 5, L, L, pp)
+    def stage3(i):
+        U = unit(i, c)
+        for k in range(1, Z):
+            got(i, nz + k - 1, U.at[lax.rem(z - k + Z, Z), x, :, :, C])
+        L = U.at[:, x, :, :, C]
+        rc(i, 2 * nz + 4, L, L, xp)
+        rc(i, 2 * nz + 6, L, L, pp)
+        L = U.at[:, 1 - x, y, :, A]
+        got(i, 2 * nz + 1, L)
+        rc(i, 2 * nz + 3, L, L, yp)
+        rc(i, 2 * nz + 7, L, L, pp)
+    def stage4(i):
+        U = unit(i, c)
+        L = U.at[:, x, 1 - y, :, A]
+        got(i, 2 * nz + 2, L); rc(i, 2 * nz + 8, L, L, pp)
+        L = U.at[:, 1 - x, 1 - y, :, A]
+        got(i, 2 * nz + 3, L); rc(i, 2 * nz + 9, L, L, pp)
+        L = U.at[:, 1 - x, :, :, C]
+        got(i, 2 * nz + 4, L); rc(i, 2 * nz + 10, L, L, pp)
+    def arrived(i):
+        U = unit(i, 1 - c)
+        got(i, 2 * nz + 5, U.at[:, x, y, :, A])
+        got(i, 2 * nz + 7, U.at[:, 1 - x, y, :, A])
+        got(i, 2 * nz + 8, U.at[:, x, 1 - y, :, A])
+        got(i, 2 * nz + 9, U.at[:, 1 - x, 1 - y, :, A])
+        got(i, 2 * nz + 6, U.at[:, x, :, :, C])
+        got(i, 2 * nz + 10, U.at[:, 1 - x, :, :, C])
+    def exchange(i, first, second):
+        mine[i - 1, 0:half, :] = jnp.where(c == 0, first, second)
+        give[i - 1, 0:half, :] = jnp.where(c == 0, second, first).astype(BF)
+        pc[i] = pltpu.make_async_remote_copy(give.at[i - 1], take.at[i - 1], psend.at[i - 1], precv.at[i - 1], device_id=pp, device_id_type=MESH)
+        pc[i].start()
+
+    stage1(0)
+    vcopies = []
+    for k, d in enumerate(others):
+        cp = pltpu.make_async_remote_copy(vec_ref, vbuf.at[dp], vsend.at[k], vrecv.at[k], device_id=d, device_id_type=MESH)
+        cp.start(); vcopies.append(cp)
+    vbuf[dp] = vec_ref[...]
+    def read(ref, first, stride):
+        return jnp.concatenate([ref[pl.ds(first + j, half, stride=stride), :] for j in range(nt)], 1)
+    exchange(1, read(qkv_ref, 0, 3 * nt), read(qkv_ref, nt, 3 * nt))
+    exchange(2, read(qkv_ref, 2 * nt, 3 * nt), read(proj_ref, 0, nt))
+    def prepare_late():
+        for j in range(nt):
+            own[5, :, 128 * j:128 * j + 128] = fc2_ref[pl.ds(j, rows, stride=nt), :].astype(BF)
+            own[6, :, 128 * j:128 * j + 128] = fc2_ref[pl.ds(j + nt * rows, rows, stride=nt), :].astype(BF)
+        nat = jnp.concatenate([read(fc1_ref, nt * v, 4 * nt) for v in range(4)], 1)
+        u = unit_lanes(nat, 4, chips)
+        exchange(3, u[0], u[1])
+        exchange(4, u[2], u[3])
+
+    emitted = []
+    def emit(src, dst):
+        cp = pltpu.make_async_copy(src, dst, osem.at[len(emitted)])
+        cp.start(); emitted.append(cp)
+    def weight(n, ref):
+        cp = pltpu.make_async_copy(ref, wbuf.at[n % 2], wsem.at[n % 2])
+        cp.start()
+        return cp
+    def both_skip(ref, k):
+        for i in range(Z // 2):
+            pltpu.make_async_copy(ref.at[k * (Z // 2) + i], wbuf.at[k, pl.ds(2 * i, 2)], wsem.at[k]).start()
+    def weight_wait(k):
+        pltpu.make_async_copy(wbuf.at[k], wbuf.at[k], wsem.at[k]).wait()
+    def cols(k, l):
+        return wbuf[k, :, :, :, :, l].reshape(wide, SPLIT)
+    def lanes_loop(fn):
+        def one(n, carry):
+            fn(pl.ds(pl.multiple_of(n * SPLIT, 128), SPLIT))
+            return carry
+        lax.fori_loop(0, wide // SPLIT, one, 0)
+    def vector(n):
+        return vecs[0:1, n * wide:(n + 1) * wide]
+    def norm(src, gain, shift, dst):
+        def one(r):
+            v = src[r, :]
+            cen = v - jnp.mean(v, -1, keepdims=True)
+            s = jnp.mean(cen * cen, -1, keepdims=True)
+            dst[r, :] = (cen * lax.rsqrt(s + epsilon) * gain + shift).astype(BF)
+        row_loop(padded, 16, one)
+    def inputs():
+        for cp in loads: cp.wait()
+        tail = padded - 16
+        jn[tail:padded, :] = jnp.zeros((16, 2 * wide), BF)
+        gm[tail:padded, :] = jnp.zeros((16, wide), BF)
+        full = length // 16 * 16
+        def one(r):
+            jn[r, 0:wide] = xin[0, r, :].astype(BF)
+            jn[r, wide:2 * wide] = xin[1, r, :].astype(BF)
+            gm[r, :] = gin[r, :].astype(BF)
+        row_loop(full, 16, one)
+        if length > full:
+            r = slice(full, length)
+            jn[r, 0:wide] = xin[0, r, :].astype(BF)
+            jn[r, wide:2 * wide] = xin[1, r, :].astype(BF)
+            gm[r, :] = gin[r, :].astype(BF)
+        def two(r):
+            u = unit_lanes(jn[r, :], 2, chips)
+            jp[0, r, :] = u[0]
+            jp[1, r, :] = u[1]
+        row_loop(padded, 16, two)
+        emit(jp, j_o)
+        emit(gm, gm_o)
+    def vectors():
+        for k in range(len(others)):
+            pltpu.make_async_remote_copy(vec_ref, vbuf.at[lax.rem(dp - (k + 1) + ndp, ndp)], vsend.at[k], vrecv.at[k], device_id=pp, device_id_type=MESH).wait_recv()
+        vecs[...] = jnp.concatenate([vbuf[k] for k in range(ndp)], 1)
+        b = unit_lanes(vecs[0:1, 7 * wide:11 * wide], 4, chips)
+        for u in range(4): b1s[u] = b[u]
+    def first_part():
+        arrived(0)
+        for k in range(2): both_skip(skip_o, k)
+        for k in range(2): weight_wait(k)
+        def one(l):
+            v = jnp.dot(jn[:, 0:wide], cols(0, l), preferred_element_type=F32)
+            v = v + jnp.dot(jn[:, wide:2 * wide], cols(1, l), preferred_element_type=F32)
+            h0[:, l] = v + vecs[0:1, pl.ds(4 * wide + l.start, SPLIT)]
+        lanes_loop(one)
+        norm(h0, vector(0), vector(1), a)
+        emit(h0, h0_o)
+        emit(a, a_o)
+    def project(n, u):
+        def one(l):
+            t[u, :, l] = jnp.dot(a[...], cols(n % 2, l), preferred_element_type=F32).astype(BF)
+        lanes_loop(one)
+    def query_keys():
+        arrived(1)
+        w = [weight(u, qp_o.at[u]) for u in range(2)]
+        for u in range(2):
+            w[u].wait()
+            project(u, u)
+    def values():
+        arrived(2)
+        w = [weight(0, qp_o.at[2]), weight(1, qp_o.at[3])]
+        for cp in w: cp.wait()
+        project(0, 2)
+        emit(t, t_o)
+    hd = wide // HEADS
+    def attend(first, last):
+        cap = cap_ref[0]
+        key = lax.broadcasted_iota(jnp.int32, (1, padded), 1)
+        live = ((key < 1 + cap) | (key >= 1 + CAPTION)) & (key < length)
+        def head(h, carry):
+            base = pl.multiple_of(jnp.minimum((h * hd) // 128, nt - 2) * 128, 128)
+            win = pl.ds(base, 256)
+            lane = lax.broadcasted_iota(jnp.int32, (1, 256), 1) + (base - h * hd)
+            inside = (lane >= 0) & (lane < hd)
+            q = jnp.where(inside, t[0, :, win].astype(F32), 0.0).astype(BF)
+            s = lax.dot_general(q, t[1, :, win], (((1,), (1,)), ((), ())), preferred_element_type=F32) * hd ** (-0.5)
+            s = jnp.where(live, s, masked_value)
+            e = jnp.exp(s - jnp.max(s, -1, keepdims=True))
+            p = (e / jnp.sum(e, -1, keepdims=True)).astype(BF)
+            v = jnp.dot(p, t[2, :, win], preferred_element_type=F32)
+            oacc[:, win] = jnp.where(inside, v, oacc[:, win])
+            return carry
+        lax.fori_loop(first, last, head, 0)
+    def second_part():
+        def cast(r): mix[r, :] = oacc[r, :].astype(BF)
+        row_loop(padded, 16, cast)
+        emit(mix, mix_o)
+        def one(l):
+            v = jnp.dot(mix[...], cols(1, l), preferred_element_type=F32)
+            h1[:, l] = h0[:, l] + (v + vecs[0:1, pl.ds(5 * wide + l.start, SPLIT)])
+        lanes_loop(one)
+        norm(h1, vector(2), vector(3), m)
+        emit(h1, h1_o)
+        emit(m, m_o)
+        def start(r): acc[r, :] = h1[r, :] + vector(6)
+        row_loop(padded, 16, start)
+    def widen_load(i):
+        arrived(i)
+        return [weight(k, fc1_o.at[2 * (i - 3) + k]) for k in range(2)]
+    def widen(u, w):
+        w[u % 2].wait()
+        def one(l):
+            tmp[:, l] = jnp.dot(m[...], cols(u % 2, l), preferred_element_type=F32)
+        lanes_loop(one)
+        def two(r):
+            v = tmp[r, :] + b1s[u]
+            cdf = 0.5 * (1.0 + lax.erf(v * 0.7071067811865476))
+            pdf = jnp.exp(-0.5 * v * v) * 0.3989422804014327
+            zz[u, r, :] = (v * cdf).astype(BF)
+            der[u, r, :] = cdf + v * pdf
+        row_loop(padded, 16, two)
+    def narrow(i):
+        arrived(i)
+        us = [i - 5, 2 + i - 5]
+        w = [weight(k, fc2_o.at[us[k]]) for k in range(2)]
+        for k in range(2):
+            w[k].wait()
+            u = us[k]
+            def one(l):
+                w = cols(k, l)
+                acc[:, l] += jnp.dot(zz[u], w, preferred_element_type=F32)
+                tmp[...] += lax.dot_general(gm[:, l], w, (((1,), (1,)), ((), ())), preferred_element_type=F32)
+            tmp[...] = jnp.zeros_like(tmp)
+            lanes_loop(one)
+            def two(r):
+                gu[u, r, :] = (tmp[r, :] * der[u, r, :]).astype(BF)
+            row_loop(padded, 16, two)
+
+    stage2(0)
+    prepare_late()
+    stage1(1)
+    stage3(0)
+    inputs()
+    vectors()
+    stage2(1); stage1(2)
+    stage3(1); stage4(0)
+    first_part()
+    stage2(2); stage1(3)
+    stage3(2); stage4(1)
+    query_keys()
+    stage2(3); stage1(4)
+    stage3(3); stage4(2)
+    oacc[...] = jnp.zeros_like(oacc)
+    values()
+    attend(0, 4)
+    stage2(4); stage1(5)
+    attend(4, 11)
+    stage3(4); stage4(3)
+    attend(11, 16)
+    second_part()
+    stage2(5); stage1(6)
+    w = widen_load(3)
+    widen(0, w)
+    stage3(5); stage4(4)
+    widen(1, w)
+    stage2(6)
+    w = widen_load(4)
+    widen(2, w)
+    stage3(6); stage4(5)
+    widen(3, w)
+    emit(zz, z_o)
+    narrow(5)
+    stage4(6)
+    narrow(6)
+    emit(gu, gu_o)
+    full = length // 16 * 16
+    def last(r): gin[r, :] = acc[r, :]
+    row_loop(full, 16, last)
+    if length > full: gin[full:length, :] = acc[full:length, :]
+    emit(gin, out_o)
+    emit(vecs, vec_o)
+    for cp in emitted: cp.wait()
+    for cp in waits: cp.wait_send()
+    for cp in pc.values(): cp.wait_send()
+    for cp in vcopies: cp.wait_send()
+
+
+def forward(cap, skip, qkv, proj, fc1, fc2, vectors, block_in, skip_in, out_grad, dpn):
+    length, wide = block_in.shape
+    Z = dpn // 2; rows = skip.shape[0] // wide
+    padded = -(-length // 16) * 16
+    lanes_a = (wide // 128 * 2 + 1) // 3 * 128
+    U = (Z, 2, 2, rows, wide)
+    hbm = pl.BlockSpec(memory_space=pl.ANY); vm = pl.BlockSpec(memory_space=pltpu.VMEM)
+    ns = 2 * (Z - 1) + 11
+    nv = vectors.shape[0]
+    D = pltpu.SemaphoreType.DMA
+    V = pltpu.VMEM
+    half = -(-rows // 2 // 16) * 16
+    S = jax.ShapeDtypeStruct
+    act = (padded, wide)
+    return pl.pallas_call(
+        functools.partial(forward_kernel, Z, wide, rows, lanes_a, length, padded),
+        out_shape=(S((Z, 2, 2, 2, rows, wide), BF), S((4,) + U, BF), S((4,) + U, BF), S((4,) + U, BF), S((1, nv * dpn), F32),
+                   S((length, wide), F32), S((2,) + act, BF), S(act, F32), S(act, BF), S((3,) + act, BF), S(act, BF), S(act, F32), S(act, BF),
+                   S((4,) + act, BF), S(act, BF), S((4,) + act, BF)),
+        in_specs=[pl.BlockSpec(memory_space=pltpu.SMEM)] + [vm] * 6 + [hbm] * 3, out_specs=(hbm,) * 16,
+        scratch_shapes=[V((7, rows, wide), BF), V((4, half, wide), F32), V((4, half, wide), BF), V((4, half, wide), BF),
+                        V((dpn, 1, nv), F32), V((1, nv * dpn), F32), V((4, 1, wide), F32), V((2, length, wide), F32), V((length, wide), F32),
+                        V((padded, 2 * wide), BF), V((2,) + act, BF), V(act, F32), V(act, BF), V((3,) + act, BF), V(act, F32), V(act, BF), V(act, F32), V(act, BF),
+                        V((4,) + act, BF), V((4,) + act, F32), V(act, BF), V((4,) + act, BF), V(act, F32), V(act, F32), V((2,) + U, BF),
+                        D((7, ns)), D((7, ns)), D((7,)), D((4,)), D((4,)), D((dpn - 1,)), D((dpn - 1,)), D((3,)), D((12,)), D((2,))],
+        compiler_params=pltpu.CompilerParams(collective_id=0, has_side_effects=True, vmem_limit_bytes=60 << 20),
+        name="forward",
+    )(cap, *(w.reshape(-1, 128) for w in (skip, qkv, proj, fc1, fc2)), vectors.reshape(1, nv), block_in, skip_in, out_grad)
+
+
+def natural_lanes(units, chips):
+    seg = units[0].shape[1] // chips
+    return jnp.concatenate([u[:, s * seg : (s + 1) * seg] for s in range(chips) for u in units], 1)
+
+
+def backward_kernel(Z, wide, rows, lanes_a, length, padded,
+                    cap_ref, vec_ref, skip_ref, qp_ref, fc1_ref, og_ref, j_ref, h0_ref, a_ref, t_ref, mix_ref, h1_ref, m_ref, z_ref, gm_ref, gu_ref,
+                    in_o, sk_o, skip_o, qkv_o, proj_o, fc1_o, fc2_o, vec_o,
+                    left, right, part, ra1, ra2, ra3, rc1, rc2, rc3, keep, give, take, vpart, vgot, vall,
+                    gin, hid, gsum, dacc, out2, gus, t, do, ga, dt, g0, sums, gacc, wbuf,
+                    xlsem, xsend, xrecv, send, recv, psend, precv, vsend, vrecv, wsend, wrecv, isem, usem, wsem, osem, free):
+    dp = lax.axis_index("dp"); f = lax.axis_index("fsdp")
+    z = dp // 2; x = dp % 2; y = f // 2; c = f % 2
+    nt = wide // 128
+    half = rows // 2
+    chips = 4 * Z
+    A = pl.ds(0, lanes_a); C = pl.ds(lanes_a, wide - lanes_a)
+    zi = [lax.rem(z + k, Z) for k in range(1, Z)]
+    zs = [(i * 2 + x, f) for i in zi]
+    xp = (z * 2 + 1 - x, f)
+    yp = (dp, (1 - y) * 2 + c)
+    pp = (dp, y * 2 + 1 - c)
+    ndp = 2 * Z
+    dps = [(lax.rem(dp + k, ndp), f) for k in range(1, ndp)]
+    fs = [(dp, lax.rem(f + k, 4)) for k in range(1, 4)]
+    bar = pltpu.get_barrier_semaphore()
+    for d in dps + fs:
+        pl.semaphore_signal(bar, inc=1, device_id=d, device_id_type=MESH)
+
+    own_rows = pl.ds(0, padded); other_rows = pl.ds(padded, padded)
+    o = 1 - c
+    locals_ = {}
+    def mine(n, src, dst):
+        cp = pltpu.make_async_copy(src, dst.at[own_rows], xlsem.at[n]); cp.start()
+        locals_[n] = cp
+    def theirs(n, src, dst):
+        cp = pltpu.make_async_remote_copy(src, dst.at[other_rows], xsend.at[n], xrecv.at[n], device_id=pp, device_id_type=MESH)
+        cp.start(); locals_[n + 100] = cp
+    early = [
+        (0, z_ref.at[2 * c], z_ref.at[2 * o], left.at[0]),
+        (1, gm_ref, gm_ref, right.at[0]),
+        (2, z_ref.at[2 * c + 1], z_ref.at[2 * o + 1], left.at[1]),
+        (3, m_ref, m_ref, left.at[2]),
+        (4, gu_ref.at[c], gu_ref.at[o], right.at[1]),
+        (5, gu_ref.at[2 + c], gu_ref.at[2 + o], right.at[2]),
+    ]
+    for n, s, _, d in early: mine(n, s, d)
+    loads = [
+        pltpu.make_async_copy(og_ref, gin, isem.at[0]),
+        pltpu.make_async_copy(h1_ref, hid, isem.at[1]),
+        pltpu.make_async_copy(t_ref, t, isem.at[2]),
+    ]
+    for cp in loads: cp.start()
+    pl.semaphore_wait(bar, len(dps) + len(fs))
+    for n, _, s, d in early: theirs(n, s, d)
+    need = [(0, 1), (2,), (3, 4), (5,), (6, 7), (8, 9), (10, 11)]
+    which = [(0, 0), (1, 0), (2, 1), (2, 2), (0, 0), (1, 1), (2, 2)]
+
+    started = {j: [] for j in range(7)}
+    def rc(j, slot, src, dst, dev):
+        cp = pltpu.make_async_remote_copy(src, dst, send.at[j, slot], recv.at[j, slot], device_id=dev, device_id_type=MESH)
+        cp.start(); started[j].append(cp)
+    def got(j, slot, dst):
+        pltpu.make_async_remote_copy(dst, dst, send.at[j, slot], recv.at[j, slot], device_id=pp, device_id_type=MESH).wait_recv()
+    nz = Z - 1
+    nb = 4
+
+    def stage1(j):
+        for n in need[j]:
+            if n in (6, 7):
+                pltpu.make_async_copy(gm_ref, left.at[0, own_rows], xlsem.at[n]).wait()
+                pltpu.make_async_remote_copy(gm_ref, left.at[0, other_rows], xsend.at[n], xrecv.at[n], device_id=pp, device_id_type=MESH).wait_recv()
+            else:
+                locals_[n].wait(); locals_[n + 100].wait_recv()
+        if j >= nb:
+            for cp in started[j - nb]: cp.wait_send()
+        D = part.at[j % nb]
+        li, ri = which[j]
+        step = wide - lanes_a
+        def chunk(n, carry):
+            lanes = pl.ds(pl.multiple_of(n * step, 128), step)
+            r = lax.dot_general(left[li], right[ri, :, lanes], (((0,), (0,)), ((), ())), preferred_element_type=F32)
+            D[:, :, :, :, lanes] = r.reshape(Z, 2, 2, rows, step).astype(BF)
+            return carry
+        lax.fori_loop(0, wide // step, chunk, 0)
+        b = j % nb
+        rc(j, 0, D.at[:, 1 - x, 1 - y, :, A], ra1.at[b, 0], yp)
+        rc(j, 2, D.at[:, 1 - x, :, :, C], rc1.at[b], xp)
+        rc(j, 1, D.at[:, x, 1 - y, :, A], ra1.at[b, 1], yp)
+    def stage2(j):
+        b = j % nb
+        D = part.at[b]
+        got(j, 0, ra1.at[b, 0])
+        for zz in range(Z):
+            va = D.at[zz, 1 - x, y, :, A]
+            va[...] = (va[...].astype(F32) + ra1[b, 0, zz].astype(F32)).astype(BF)
+        rc(j, 3, D.at[:, 1 - x, y, :, A], ra2.at[b], xp)
+        got(j, 2, rc1.at[b])
+        for zz in range(Z):
+            for yy in range(2):
+                va = D.at[zz, x, yy, :, C]
+                va[...] = (va[...].astype(F32) + rc1[b, zz, yy].astype(F32)).astype(BF)
+        for k in range(nz):
+            rc(j, 4 + k, D.at[zi[k], x, :, :, C], rc2.at[b, k], zs[k])
+    def stage3(j):
+        b = j % nb
+        D = part.at[b]
+        got(j, 1, ra1.at[b, 1])
+        got(j, 3, ra2.at[b])
+        for zz in range(Z):
+            va = D.at[zz, x, y, :, A]
+            va[...] = (va[...].astype(F32) + ra1[b, 1, zz].astype(F32) + ra2[b, zz].astype(F32)).astype(BF)
+        for k in range(nz):
+            rc(j, 4 + nz + k, D.at[zi[k], x, y, :, A], ra3.at[b, k], zs[k])
+        for k in range(nz):
+            got(j, 4 + k, rc2.at[b, k])
+        for yy in range(2):
+            va = D.at[z, x, yy, :, C]
+            s = va[...].astype(F32)
+            for k in range(nz):
+                s = s + rc2[b, k, yy].astype(F32)
+            va[...] = s.astype(BF)
+        rc(j, 4 + 2 * nz, D.at[z, x, 1 - y, :, C], rc3.at[b], yp)
+    pcopies = {}
+    def lay(ref, val, first, stride, n):
+        for i in range(val.shape[1] // 128):
+            ref[pl.ds(first + i, n, stride=stride), :] = val[:, 128 * i:128 * i + 128]
+    def stage4(j):
+        b = j % nb
+        D = part.at[b]
+        for k in range(nz):
+            got(j, 4 + nz + k, ra3.at[b, k])
+        got(j, 4 + 2 * nz, rc3.at[b])
+        p = D[z, x, y, :, 0:lanes_a].astype(F32)
+        for k in range(nz):
+            p = p + ra3[b, k].astype(F32)
+        q = D[z, x, y, :, lanes_a:wide].astype(F32) + rc3[b].astype(F32)
+        v = jnp.concatenate([p, q], 1)
+        if j in (0, 1):
+            lay(fc2_o, v, j * rows * nt, nt, rows)
+        elif j == 6:
+            lay(skip_o, v, 0, nt, rows)
+        else:
+            lo = v[0:half]; hi = v[half:rows]
+            keep[j - 2, 0:half, :] = jnp.where(c == 0, lo, hi)
+            give[j - 2, 0:half, :] = jnp.where(c == 0, hi, lo)
+            cp = pltpu.make_async_remote_copy(give.at[j - 2], take.at[j - 2], psend.at[j - 2], precv.at[j - 2], device_id=pp, device_id_type=MESH)
+            cp.start(); pcopies[j] = cp
+    def both(j):
+        pcopies[j].wait_recv()
+        p = keep[j - 2, 0:half, :]; q = take[j - 2, 0:half, :]
+        return jnp.where(c == 0, p, q), jnp.where(c == 0, q, p)
+    def stage5(j):
+        if j == 3:
+            lay(fc1_o, natural_lanes(both(2) + both(3), chips), 0, 4 * nt, half)
+        elif j == 5:
+            first, second = both(5)
+            lay(qkv_o, first, 0, 3 * nt, half)
+            lay(qkv_o, second, nt, 3 * nt, half)
+        elif j == 4:
+            first, second = both(4)
+            lay(qkv_o, first, 2 * nt, 3 * nt, half)
+            lay(proj_o, second, 0, nt, half)
+
+    def weight(n, ref):
+        cp = pltpu.make_async_copy(ref, wbuf.at[n % 2], wsem.at[n % 2])
+        cp.start()
+        return cp
+    def both_skip(ref, k):
+        for i in range(Z // 2):
+            pltpu.make_async_copy(ref.at[k * (Z // 2) + i], wbuf.at[k, pl.ds(2 * i, 2)], wsem.at[k]).start()
+    def weight_wait(k):
+        pltpu.make_async_copy(wbuf.at[k], wbuf.at[k], wsem.at[k]).wait()
+    def cols(k, l):
+        return wbuf[k, :, :, :, :, l].reshape(wide, SPLIT)
+    def lanes_loop(fn):
+        def one(n, carry):
+            fn(pl.ds(pl.multiple_of(n * SPLIT, 128), SPLIT))
+            return carry
+        lax.fori_loop(0, wide // SPLIT, one, 0)
+    def vector(n):
+        return vec_ref[0:1, n * wide:(n + 1) * wide]
+    def zero(n): gacc[n] = jnp.zeros((8, wide), F32)
+    def add_rows(n, v):
+        gacc[n] += v[0:8] + v[8:16]
+    def close(n):
+        return jnp.sum(gacc[n], 0, keepdims=True)
+    def norm_back(dy, src, gain, fn):
+        zero(0); zero(1); zero(2)
+        def one(r):
+            d = dy[r, :]
+            v = src[r, :]
+            cen = v - jnp.mean(v, -1, keepdims=True)
+            rs = lax.rsqrt(jnp.mean(cen * cen, -1, keepdims=True) + epsilon)
+            xh = cen * rs
+            dx = d * gain
+            g = rs * (dx - jnp.mean(dx, -1, keepdims=True) - xh * jnp.mean(dx * xh, -1, keepdims=True))
+            add_rows(0, d * xh)
+            add_rows(1, d)
+            fn(r, g)
+        row_loop(padded, 16, one)
+    def turned(dst, lhs, n, fresh):
+        if fresh: dst[...] = jnp.zeros_like(dst)
+        def one(l):
+            dst[...] += lax.dot_general(lhs[:, l], cols(n, l), (((1,), (1,)), ((), ())), preferred_element_type=F32)
+        lanes_loop(one)
+    def widen_back():
+        def load(u):
+            cp = pltpu.make_async_copy(gu_ref.at[u], gus.at[u % 2], usem.at[u % 2]); cp.start()
+            return (cp, weight(u, fc1_ref.at[u]))
+        w = [load(0), load(1)]
+        for u in range(4):
+            for cp in w[u]: cp.wait()
+            turned(dacc, gus.at[u % 2], u % 2, u == 0)
+            zero(0)
+            def one(r): add_rows(0, gus[u % 2, r, :].astype(F32))
+            row_loop(padded, 16, one)
+            sums[7 + u] = close(0)
+            if u < 2: w.append(load(u + 2))
+    def norm_two():
+        weight(0, qp_ref.at[3])
+        for cp in loads: cp.wait()
+        full = length // 16 * 16
+        if padded > full:
+            gsum[padded - 16:padded, :] = jnp.zeros((16, wide), F32)
+        def copy(r): gsum[r, :] = gin[r, :]
+        row_loop(full, 16, copy)
+        if length > full: gsum[full:length, :] = gin[full:length, :]
+        def fn(r, g):
+            s = gsum[r, :] + g
+            gsum[r, :] = s
+            b = s.astype(BF)
+            ga[r, :] = b
+            add_rows(2, b.astype(F32))
+        norm_back(dacc, hid, vector(2), fn)
+        sums[2] = close(0); sums[3] = close(1); sums[5] = close(2)
+        pltpu.make_async_copy(h0_ref, hid, isem.at[1]).start()
+        zero(0)
+        def one(r): add_rows(0, right[0, r, :].astype(F32))
+        row_loop(padded, 16, one)
+        sums[6] = close(0)
+        pltpu.make_async_copy(qp_ref.at[3], wbuf.at[0], wsem.at[0]).wait()
+        turned(dacc, ga, 0, True)
+        def two(r): do[r, :] = dacc[r, :].astype(BF)
+        row_loop(padded, 16, two)
+    hd = wide // HEADS
+    def attend(first, last):
+        cap = cap_ref[0]
+        key = lax.broadcasted_iota(jnp.int32, (padded, 1), 0)
+        live = ((key < 1 + cap) | (key >= 1 + CAPTION)) & (key < length)
+        def head(h, carry):
+            base = pl.multiple_of(jnp.minimum((h * hd) // 128, nt - 2) * 128, 128)
+            win = pl.ds(base, 256)
+            lane = lax.broadcasted_iota(jnp.int32, (1, 256), 1) + (base - h * hd)
+            inside = (lane >= 0) & (lane < hd)
+            q = jnp.where(inside, t[0, :, win].astype(F32), 0.0).astype(BF)
+            k = t[1, :, win]
+            g = jnp.where(inside, do[:, win].astype(F32), 0.0).astype(BF)
+            s = lax.dot_general(k, q, (((1,), (1,)), ((), ())), preferred_element_type=F32) * hd ** (-0.5)
+            s = jnp.where(live, s, masked_value)
+            e = jnp.exp(s - jnp.max(s, 0, keepdims=True))
+            p = e * (1.0 / jnp.sum(e, 0, keepdims=True))
+            d = lax.dot_general(t[2, :, win], g, (((1,), (1,)), ((), ())), preferred_element_type=F32)
+            ds = (p * (d - jnp.sum(p * d, 0, keepdims=True))).astype(BF)
+            dq = lax.dot_general(ds, k, (((0,), (0,)), ((), ())), preferred_element_type=F32) * hd ** (-0.5)
+            dk = jnp.dot(ds, q, preferred_element_type=F32) * hd ** (-0.5)
+            dv = jnp.dot(p.astype(BF), g, preferred_element_type=F32)
+            for i, v in enumerate((dq, dk, dv)):
+                dt[i, :, win] = jnp.where(inside, v, dt[i, :, win].astype(F32)).astype(BF)
+            return carry
+        lax.fori_loop(first, last, head, 0)
+    def late_left():
+        pl.semaphore_signal(free, inc=1, device_id=pp, device_id_type=MESH)
+        pl.semaphore_wait(free, 1)
+        @pl.when(c == 0)
+        def _():
+            pltpu.make_async_copy(a_ref, left.at[0, own_rows], xlsem.at[6]).start()
+            pltpu.make_async_remote_copy(mix_ref, left.at[0, other_rows], xsend.at[6], xrecv.at[6], device_id=pp, device_id_type=MESH).start()
+        @pl.when(c == 1)
+        def _():
+            pltpu.make_async_copy(mix_ref, left.at[0, own_rows], xlsem.at[6]).start()
+            pltpu.make_async_remote_copy(a_ref, left.at[0, other_rows], xsend.at[6], xrecv.at[6], device_id=pp, device_id_type=MESH).start()
+        mine(8, a_ref, left.at[1]); theirs(8, a_ref, left.at[1])
+        mine(10, j_ref.at[c], left.at[2]); theirs(10, j_ref.at[o], left.at[2])
+    def late_right():
+        @pl.when(c == 0)
+        def _():
+            pltpu.make_async_copy(dt.at[2], right.at[0, own_rows], xlsem.at[7]).start()
+            pltpu.make_async_remote_copy(ga, right.at[0, other_rows], xsend.at[7], xrecv.at[7], device_id=pp, device_id_type=MESH).start()
+        @pl.when(c == 1)
+        def _():
+            pltpu.make_async_copy(ga, right.at[0, own_rows], xlsem.at[7]).start()
+            pltpu.make_async_remote_copy(dt.at[2], right.at[0, other_rows], xsend.at[7], xrecv.at[7], device_id=pp, device_id_type=MESH).start()
+        mine(9, dt.at[c], right.at[1]); theirs(9, dt.at[o], right.at[1])
+    def project_back():
+        w = [weight(0, qp_ref.at[0]), weight(1, qp_ref.at[1])]
+        for i in range(3):
+            w[i].wait()
+            turned(dacc, dt.at[i], i % 2, i == 0)
+            if i == 0: w.append(weight(2, qp_ref.at[2]))
+    def norm_one():
+        pltpu.make_async_copy(h0_ref, hid, isem.at[1]).wait()
+        def fn(r, g):
+            b = (gsum[r, :] + g).astype(BF)
+            g0[r, :] = b
+            add_rows(2, b.astype(F32))
+        norm_back(dacc, hid, vector(0), fn)
+        sums[0] = close(0); sums[1] = close(1); sums[4] = close(2)
+        mine(11, g0, right.at[2]); theirs(11, g0, right.at[2])
+    def join_back():
+        for k in range(2): both_skip(skip_ref, k)
+        full = length // 16 * 16
+        for i, (dst, out) in enumerate(((gin, in_o), (out2, sk_o))):
+            weight_wait(i)
+            turned(dacc, g0, i, True)
+            def copy(r): dst[r, :] = dacc[r, :]
+            row_loop(full, 16, copy)
+            if length > full: dst[full:length, :] = dacc[full:length, :]
+            pltpu.make_async_copy(dst, out, osem.at[i]).start()
+    vcopies = []
+    nv = vpart.shape[2]
+    def vec_send():
+        full = jnp.concatenate([sums[i] for i in range(7)] + [natural_lanes([sums[7 + u] for u in range(4)], chips)], 1)
+        for k in range(ndp): vpart[k] = full[:, k * nv:(k + 1) * nv]
+        for k, d in enumerate(dps):
+            cp = pltpu.make_async_remote_copy(vpart.at[d[0]], vgot.at[k], vsend.at[k], vrecv.at[k], device_id=d, device_id_type=MESH)
+            cp.start(); vcopies.append(cp)
+    def vec_first():
+        s = vpart[dp]
+        for k in range(len(dps)):
+            pltpu.make_async_remote_copy(vgot.at[k], vgot.at[k], vsend.at[k], vrecv.at[k], device_id=pp, device_id_type=MESH).wait_recv()
+            s = s + vgot[k]
+        vall[f] = s
+        for k, d in enumerate(fs):
+            cp = pltpu.make_async_remote_copy(vall.at[f], vall.at[f], wsend.at[k], wrecv.at[k], device_id=d, device_id_type=MESH)
+            cp.start(); vcopies.append(cp)
+    def vec_last():
+        for k in range(3):
+            src = lax.rem(f - (k + 1) + 4, 4)
+            pltpu.make_async_remote_copy(vall.at[src], vall.at[src], wsend.at[k], wrecv.at[k], device_id=pp, device_id_type=MESH).wait_recv()
+        vec_o[...] = vall[0] + vall[1] + vall[2] + vall[3]
+
+    dt[...] = jnp.zeros_like(dt)
+    stage1(0)
+    widen_back()
+    stage1(1); stage2(0)
+    norm_two()
+    stage1(2); stage2(1); stage3(0)
+    attend(0, 4)
+    stage1(3)
+    late_left()
+    stage2(2); stage3(1); stage4(0)
+    attend(4, 10)
+    stage2(3); stage3(2); stage4(1)
+    attend(10, 16)
+    late_right()
+    stage1(4)
+    stage3(3); stage4(2)
+    stage1(5); stage2(4); stage4(3)
+    project_back()
+    norm_one()
+    vec_send()
+    stage2(5); stage3(4)
+    stage1(6)
+    vec_first()
+    join_back()
+    stage5(3)
+    stage2(6); stage3(5); stage4(4)
+    vec_last()
+    stage3(6); stage4(5); stage5(4)
+    stage5(5)
+    stage4(6)
+    for j in range(3, 7):
+        for cp in started[j]: cp.wait_send()
+    for cp in pcopies.values(): cp.wait_send()
+    for cp in vcopies: cp.wait_send()
+    for n in (0, 1, 2, 3, 4, 5, 8, 9, 10, 11): locals_[n + 100].wait_send()
+    for n in (6, 7):
+        pltpu.make_async_remote_copy(gm_ref, left.at[0, other_rows], xsend.at[n], xrecv.at[n], device_id=pp, device_id_type=MESH).wait_send()
+    pltpu.make_async_copy(gin, in_o, osem.at[0]).wait()
+    pltpu.make_async_copy(out2, sk_o, osem.at[1]).wait()
+
+
+def backward(cap, vec, skip, qp, fc1, out_grad, acts, dpn):
+    length, wide = out_grad.shape
+    Z = dpn // 2; rows = 2 * wide // (4 * dpn)
+    padded = acts[1].shape[0]
+    lanes_a = (wide // 128 * 2 + 1) // 3 * 128
+    lc = wide - lanes_a
+    hbm = pl.BlockSpec(memory_space=pl.ANY); vm = pl.BlockSpec(memory_space=pltpu.VMEM)
+    D = pltpu.SemaphoreType.DMA
+    half = rows // 2; hp = -(-half // 8) * 8
+    nv = vec.shape[1] // dpn
+    nz = Z - 1; ns = 5 + 2 * nz
+    nb = 4
+    V = pltpu.VMEM
+    S = jax.ShapeDtypeStruct
+    act = (padded, wide)
+    outs = [rows * wide // 128, 3 * half * wide // 128, half * wide // 128, 4 * half * wide // 128, 2 * rows * wide // 128]
+    res = pl.pallas_call(
+        functools.partial(backward_kernel, Z, wide, rows, lanes_a, length, padded),
+        out_shape=(S((length, wide), F32),) * 2 + tuple(S((n, 128), F32) for n in outs) + (S((1, nv), F32),),
+        in_specs=[pl.BlockSpec(memory_space=pltpu.SMEM), vm] + [hbm] * 14, out_specs=(hbm,) * 2 + (vm,) * 6,
+        scratch_shapes=[V((3, 2 * padded, wide), BF), V((3, 2 * padded, wide), BF), V((nb, Z, 2, 2, rows, wide), BF),
+                        V((nb, 2, Z, rows, lanes_a), BF), V((nb, Z, rows, lanes_a), BF), V((nb, nz, rows, lanes_a), BF),
+                        V((nb, Z, 2, rows, lc), BF), V((nb, nz, 2, rows, lc), BF), V((nb, rows, lc), BF),
+                        V((4, hp, wide), F32), V((4, hp, wide), F32), V((4, hp, wide), F32),
+                        V((dpn, 1, nv), F32), V((dpn - 1, 1, nv), F32), V((4, 1, nv), F32),
+                        V((length, wide), F32), V(act, F32), V(act, F32), V(act, F32), V((length, wide), F32), V((2,) + act, BF), V((3,) + act, BF),
+                        V(act, BF), V(act, BF), V((3,) + act, BF), V(act, BF), V((11, 1, wide), F32), V((3, 8, wide), F32), V((2, Z, 2, 2, rows, wide), BF),
+                        D((12,)), D((12,)), D((12,)), D((7, ns)), D((7, ns)), D((4,)), D((4,)), D((dpn - 1,)), D((dpn - 1,)), D((3,)), D((3,)),
+                        D((3,)), D((2,)), D((2,)), D((2,)), pltpu.SemaphoreType.REGULAR],
+        compiler_params=pltpu.CompilerParams(collective_id=1, has_side_effects=True, vmem_limit_bytes=63 << 20),
+        name="backward",
+    )(cap, vec, skip, qp, fc1, out_grad, *acts)
+    return res[:2] + tuple(r.reshape(-1) for r in res[2:])
+
+
+def whole_rows(width, dp, fsdp, items, heads, hidden):
+    return (
+        fsdp == 4 and dp % 2 == 0 and width % (dp * 16) == 0 and items == 1 and hidden == 4 * width
+        and width % SPLIT == 0 and width // heads <= 128
+    )
+
+
+def fast_body(block_in, skip_in, out_grad, caption_len, skip_w, qkv_w, proj_w, fc1_w, fc2_w, vectors):
+    shape = block_in.shape
+    dpn = lax.axis_size("dp")
+    res = forward(
+        caption_len, skip_w, qkv_w, proj_w, fc1_w, fc2_w, vectors,
+        block_in.reshape(shape[1:]), skip_in.reshape(shape[1:]), out_grad.reshape(shape[1:]), dpn,
+    )
+    skip_m, qp_m, fc1_m, fc2_m, vec, block_out = res[:6]
+    grads = backward(caption_len, vec, skip_m, qp_m, fc1_m, out_grad.reshape(shape[1:]), res[6:], dpn)
+    return (block_out.reshape(shape), grads[0].reshape(shape), grads[1].reshape(shape)) + tuple(grads[2:])
+
+
 def body(block_in, skip_in, out_grad, caption_len, skip_w, qkv_w, proj_w, fc1_w, fc2_w, vectors):
     items, length, width = block_in.shape
+    if whole_rows(width, lax.axis_size("dp"), lax.axis_size("fsdp"), items, HEADS, FF):
+        return fast_body(
+            block_in, skip_in, out_grad, caption_len, skip_w, qkv_w, proj_w, fc1_w, fc2_w, vectors
+        )
     heads = HEADS
     head_dim = width // heads
     hidden = FF

time: 1840 us -> 431 us (0.23)
  waiting for transfers between devices: 1100 us -> 0 us
  Pallas kernels: 0 us -> 399 us
  other arithmetic: 242 us -> 0.62 us
  local copies, waits for them, and re-layouts: 248 us -> 21 us
  matrix products: 141 us -> 0 us
  blocking collectives: 84.1 us -> 0 us
    unnamed x7 -> x0, waiting for transfers between devices: 986 us -> none
    pallas_call x0 -> x2, Pallas kernels: none -> 399 us  [the longest x1 200 us: forward(): pl.pallas_call(functools.partial(forward_kernel, Z, wide, rows, lanes_a,...]
    all_gather x2 -> x0, other arithmetic: 216 us -> none  [the longest x1 167 us: body(): lax.all_gather(qkv_w.astype(jnp.bfloat16), ('dp', 'fsdp'), axis=0, tiled=...]
    dot_general x21 -> x0, matrix products: 141 us -> none  [the longest x5 47.5 us: product(): return jnp.dot(left, right, preferred_element_type=jnp.float32)]
    all_gather x5 -> x0, waiting for transfers between devices: 116 us -> none  [the longest x1 96.3 us: body(): lax.all_gather(qkv_w.astype(jnp.bfloat16), ('dp', 'fsdp'), axis=0, tiled=...]
    another operation x5 -> x0, local copies, waits for them, and re-layouts: 79.5 us -> none  [body(): flat_piece(pair[0], pair[1])]
    unnamed x2 -> x0, blocking collectives: 77.2 us -> none
    reshape x5 -> x1, local copies, waits for them, and re-layouts: 72.3 us -> 1.3 us  [forward(): vectors.reshape(1, nv)]
  transfers between devices with their start and end apart: 6 -> 0, of which waited for: 4 -> 0; matrix products, arithmetic and copies ran while one was open for 20% -> 0% of each run, Pallas kernels for 0% -> 0%
where the time goes in v3:
time: 431 us; the launch traced here: 423 us
  Pallas kernels  399 us (93%)
  local copies, waits for them, and re-layouts  21 us (5%)
    pallas_call x1, Pallas kernels, forward(): pl.pallas_call(functools.partial(forward_kernel, Z, wide, rows, lanes_a,...  200 us
    pallas_call x1, Pallas kernels, backward(): pl.pallas_call(functools.partial(backward_kernel, Z, wide, rows, lanes_a,...  199 us
    unnamed x28, local copies, waits for them, and re-layouts  19.7 us

profile of v3, /device:TPU:0, one launch (start us, length us, event | category | flops | bytes accessed | tf_op | source)
XLA Modules:
  0.0 422.6 jit_solution(4333439202331767444)
XLA Ops:
  1.3 1.3 reshape.78.vec_ref
  2.6 0.0 copy-start.1
  2.6 0.0 copy-start.2
  2.6 2.8 copy.28
  5.4 0.0 copy-done.1
  5.4 0.0 copy-done.2
  5.4 1.9 copy_bitcast_fusion
  7.2 199.8 %forward.1 = (bf16[4,2,2,2,72,1152]{5,4,3,2,1,0:T(8,128)(2,1)}, bf16[4,4,2,2,72,1152]{5,4,3,2,1,0:T(8,128)(2,1)}, bf16[4,4,2,2,72,1152]{5,4,3,2,1,0:T(8,128)(2,1...) custom-call(s32[1]{0:T(128)S(6)} %copy.34.cap_ref, ...), custom_call_target="tpu_custom_call" | custom-call | tf_op jit(solution)/shard_map/forward/pallas_call | solution.py:427
  207.0 4.1 copy.19
  211.1 199.4 %backward.1 = (f32[334,1152]{1,0:T(8,128)}, f32[334,1152]{1,0:T(8,128)}, f32[648,128]{1,0:T(8,128)}, f32[972,128]{1,0:T(8,128)}, f32[324,128]{1,0:T(8,128)}, /*i...) custom-call(s32[1]{0:T(128)S(6)} %copy.34.cap_ref, f32[1,12672]{1,0:T(1,128)} %get-tuple-element.33.vec_ref, ...), custom_call_target="tpu_custom_call" | custom-call | tf_op jit(solution)/shard_map/backward/pallas_call | solution.py:842
  410.5 0.0 copy-start
  410.5 4.2 %copy.20 = f32[1,334,1152]{2,0,1:T(1,128)} copy(f32[1,334,1152]{2,1,0:T(8,128)} %bitcast.22) | data formatting | bytes 3078144
  414.8 0.0 copy-start.8
  414.8 0.0 copy-done
  414.8 0.0 copy-start.6
  414.8 0.0 copy-start.5
  414.8 2.7 copy.21
  417.5 0.0 copy-done.8
  417.5 0.0 copy-start.7
  417.5 0.0 copy-start.4
  417.5 0.6 reduce
  418.1 0.0 copy-done.6
  418.1 0.0 copy-start.3
  418.1 0.7 copy.35
  418.9 0.0 copy-done.5
  418.9 0.8 copy.36
  419.7 0.0 copy-done.7
  419.7 0.7 copy.37
  420.4 0.0 copy-done.4
  420.4 0.9 copy.38
  421.2 0.0 copy-done.3
  421.2 0.9 copy.39
Async XLA Ops:
  2.6 2.8 copy-start.1
  2.6 2.8 copy-start.2
  410.5 4.2 %copy-start = (f32[334,1152]{1,0:T(8,128)S(1)}, f32[334,1152]{1,0:T(8,128)}, u32[]{:S(2)}) copy-start(f32[334,1152]{1,0:T(8,128)} %get-tuple-element.48) | copy-start | bytes 4617220
  414.8 2.7 copy-start.8
  414.8 3.4 copy-start.6
  414.8 4.1 copy-start.5
  417.5 2.2 copy-start.7
  417.5 2.9 copy-start.4
  418.1 3.1 copy-start.3
